TPU v7x, 256 devices: a whole 4x4x8 slice. The times are simulated.
256 devices in a mesh: grp: 16 (over z, core), sib: 16 (over y, x).
Axes of the slice: x: 4, y: 4, z: 8, core: 2. Of those that a mesh axis runs over, the one named last changes fastest.
Arguments:
- targets: float32 [327680, 256], P(('grp', 'sib')), may hold values from -6 to 6
- leaf_order: int32 [256, 1280], P(('grp', 'sib')), may hold values from 0 to 1279, each once within a row
- near_block: float32 [327680, 1280], P(('grp', 'sib')), may hold values from -0.15625 to 0.15625
- leaf_basis: float32 [327680, 128], P(('grp', 'sib')), may hold values from -0.15625 to 0.15625
- sibling_coupling: float32 [32768, 2048], P(('grp', 'sib')), may hold values from -0.5 to 0.5
- transfer: float32 [32768, 128], P(('grp', 'sib')), may hold values from -0.5 to 0.5
- top_coupling: float32 [2048, 2048], P('grp', 'sib'), may hold values from -0.125 to 0.125
Outputs:
- coefficients: float32 [327680, 256], P(('grp', 'sib'))
- fitted: float32 [327680, 256], P(('grp', 'sib'))
Inputs may be any that keep to these rules, and one draw needn't show every extreme that they name: `leaf_order`: each row of 1280 entries holds every number of 0 to 1279 once.
All inputs are finite; a program needn't handle non-finite values.
Results may differ from a plain program's by a relative error of at most 0.00025.
Values sent between devices are 32-bit elements; how exact they have to be, the bound alone decides.
No kernel may reach another device: no remote copies, remote signals or barrier semaphores. Data moves between devices by JAX's collectives and lax.ppermute only.
A program may use at most 64 MiB of HBM per device.

v0:
```python
import functools
import math

import jax
import jax.numpy as jnp
from jax import lax
from jax.experimental import pallas as pl
from jax.experimental.pallas import tpu as pltpu
from jax.sharding import PartitionSpec as P


ITERS = 3
SIDE = 4
TILE = 256
VMEM_GRANT = 34 << 20

step_size = 0.5
shrink_rate = 0.1
f32, bf16 = jnp.float32, jnp.bfloat16


def halves(value):
    high = value.astype(bf16)
    return high, (value - high.astype(f32)).astype(bf16)


def product(left, right):
    dot = functools.partial(jnp.dot, preferred_element_type=f32)
    return dot(left[0], right[0]) + (dot(left[0], right[1]) + dot(left[1], right[0]))


def call(kernel, outs, flops, *args, near_by=0, **kwargs):
    far = len(args) - near_by
    moved = sum(v.size * v.dtype.itemsize for v in args)
    moved += sum(math.prod(shape) * jnp.dtype(kind).itemsize for shape, kind in outs)
    outs = [pltpu.HBM(*out) for out in outs]
    args = [pltpu.with_memory_space_constraint(v, pltpu.HBM) for v in args[:far]] + [*args[far:]]
    return pl.pallas_call(
        kernel,
        out_shape=outs,
        cost_estimate=pl.CostEstimate(flops=flops, bytes_accessed=moved, transcendentals=0),
        compiler_params=pltpu.CompilerParams(vmem_limit_bytes=VMEM_GRANT),
        **kwargs,
    )(*args)


def exchange(copies, axis):
    return lax.all_to_all(copies, axis, split_axis=0, concat_axis=0, tiled=True)


def shifted(value, rows, columns):
    pairs = [
        (r * SIDE + c, (r + rows) % SIDE * SIDE + (c + columns) % SIDE)
        for r in range(SIDE)
        for c in range(SIDE)
    ]
    return lax.ppermute(value, "sib", pairs)


def sibling_behind(rows, columns):
    sib = lax.axis_index("sib")
    row = lax.rem(sib // SIDE + SIDE - rows, SIDE)
    return row * SIDE + lax.rem(sib % SIDE + SIDE - columns, SIDE)


def arrange_kernel(row_ref, top_ref, own_ref, *sent_refs):
    rank = row_ref.shape[0]
    for ahead in range(SIDE):
        target = own_ref if ahead == 0 else sent_refs[ahead - 1]
        for behind in range(SIDE):
            spot = slice(behind * rank, (behind + 1) * rank)
            if ahead == 0 and behind == 0:
                target[:, spot] = jnp.zeros((rank, rank), f32)
            else:
                source = sibling_behind(SIDE - ahead, behind) if ahead else sibling_behind(0, behind)
                target[:, spot] = row_ref[:, pl.ds(pl.multiple_of(source * rank, rank), rank)]
        if ahead:
            target[:, SIDE * rank :] = top_ref[...]


def arrange(sibling_row, top_block):
    rank = top_block.shape[0]
    wide = ((rank, (SIDE + 1) * rank), f32)
    outs = [((rank, SIDE * rank), f32)] + [wide] * (SIDE - 1)
    return call(arrange_kernel, outs, 0, sibling_row, top_block)


def couple_kernel(top_ref, own_ref, *refs):
    *got, split_ref, tops_ref = refs
    rank = top_ref.shape[0]
    tops_ref[0] = top_ref[...]
    for above in range(SIDE):
        rows = slice(above * rank, (above + 1) * rank)
        block = own_ref[...] if above == 0 else got[above - 1][:, : SIDE * rank]
        split_ref[0, rows, :], split_ref[1, rows, :] = halves(block)
        if above:
            tops_ref[above] = got[above - 1][:, SIDE * rank :]


def couple(top_block, own, got):
    rank = top_block.shape[0]
    outs = [((2, SIDE * rank, SIDE * rank), bf16), ((SIDE, rank, rank), f32)]
    return call(couple_kernel, outs, 0, top_block, own, *got, near_by=SIDE - 1)


def place_kernel(*refs):
    *parts, out_ref = refs
    for behind in range(SIDE):
        for above in range(SIDE):
            owner = sibling_behind(above, behind)
            out_ref[0, owner], out_ref[1, owner] = halves(parts[behind][above].T)


def place(parts):
    _, rank, width = parts[0].shape
    return call(place_kernel, [((2, SIDE * SIDE, rank, width), bf16)], 0, *parts, near_by=SIDE - 1)[0]


def bands(rows):
    return rows // TILE


def band(index):
    return pl.ds(pl.multiple_of(index * TILE, TILE), TILE)


def over_bands(rows, body):
    lax.fori_loop(0, bands(rows), lambda k, _: body(k), None)


def copies_of(*ends):
    return [pltpu.make_async_copy(*end) for end in ends]


def start(copies):
    for copy in copies:
        copy.start()
    return copies


def finish(copies):
    for copy in copies:
        copy.wait()


def banded(pairs, sems, index):
    cut = band(index)
    return copies_of(*((a.at[cut], b.at[cut], sems.at[n, index]) for n, (a, b) in enumerate(pairs)))


def add_up(total_ref, basis, weights):
    dot = functools.partial(
        lax.dot_general, dimension_numbers=(((0,), (0,)), ((), ())), preferred_element_type=f32
    )
    part = dot(basis[0], weights[0]) + (dot(basis[0], weights[1]) + dot(basis[1], weights[0]))
    total_ref[...] += part


def send_up(total_ref, leaf, group, leaf_ref, group_ref, sems):
    rank = leaf.shape[0]
    leaf[...] = total_ref[:rank, :]
    group[...] = total_ref[rank:, :].T
    return start(copies_of((leaf, leaf_ref, sems.at[0]), (group, group_ref, sems.at[1])))


HBM = pl.BlockSpec(memory_space=pltpu.HBM)
VMEM = pl.BlockSpec(memory_space=pltpu.VMEM)
DMA = pltpu.SemaphoreType.DMA


def begin_kernel(targets_ref, basis_ref, transfer_ref, *refs):
    split_ref, leaf_ref, group_ref, targets, basis, split, total, leaf, group, *sems = refs
    in_sems, out_sems, end_sems = sems
    rows = basis.shape[0]
    pairs = ((targets_ref, targets), (basis_ref, basis))
    outgoing = ((split.at[0], split_ref.at[0]), (split.at[1], split_ref.at[1]))
    over_bands(rows, lambda k: (start(banded(pairs, in_sems, k)), None)[1])
    transfer = halves(transfer_ref[...])
    total[...] = jnp.zeros_like(total)

    def step(k):
        cut = band(k)
        finish(banded(pairs, in_sems, k))
        both = jnp.concatenate([basis[cut, :], product(halves(basis[cut, :]), transfer)], axis=1)
        high, low = halves(both)
        split[0, cut, :] = high
        split[1, cut, :] = low
        start(banded(outgoing, out_sems, k))
        add_up(total, (high, low), halves(step_size * targets[cut, :]))

    over_bands(rows, step)
    sent = send_up(total, leaf, group, leaf_ref, group_ref, end_sems)
    over_bands(rows, lambda k: finish(banded(outgoing, out_sems, k)))
    finish(sent)


def begin(tree_targets, basis, transfer):
    rows, columns = tree_targets.shape
    rank = transfer.shape[0]
    outs = [((2, rows, 2 * rank), bf16), ((rank, columns), f32), ((columns, rank), f32)]
    return call(
        begin_kernel,
        outs,
        18 * rows * columns * rank,
        tree_targets,
        basis,
        transfer,
        in_specs=[HBM, HBM, VMEM],
        near_by=1,
        out_specs=[HBM] * 3,
        scratch_shapes=[
            pltpu.VMEM((rows, columns), f32),
            pltpu.VMEM((rows, rank), f32),
            pltpu.VMEM(*outs[0]),
            pltpu.VMEM((2 * rank, columns), f32),
            *(pltpu.VMEM(*out) for out in outs[1:]),
            DMA((2, bands(rows))),
            DMA((2, bands(rows))),
            DMA((2,)),
        ],
    )


def fit_kernel(last, *refs):
    sum_ref, base_ref, along_ref, root_ref, *refs = refs
    if last:
        order_ref, coeffs_ref, fitted_ref, sums, base, along, split, in_sems, out_sems = refs
        outgoing = ((sums, coeffs_ref), (base, fitted_ref))
    else:
        coeffs_ref, leaf_ref, group_ref, sums, base, along, *refs = refs
        total, leaf, group, in_sems, out_sems, end_sems = refs
        total[...] = jnp.zeros_like(total)
        outgoing = ((base, coeffs_ref),)
    rows, columns = sums.shape
    rank = root_ref.shape[1]
    pairs = ((sum_ref, sums), (base_ref, base))
    pairs += ((along_ref.at[0], along.at[0]), (along_ref.at[1], along.at[1]))
    over_bands(rows, lambda k: (start(banded(pairs, in_sems, k)), None)[1])
    root = halves(root_ref[...].T)

    def step(k):
        cut = band(k)
        finish(banded(pairs, in_sems, k))
        high, low = along[0, cut, :], along[1, cut, :]
        fitted = jnp.tanh(sums[cut, :] + product((along[0, cut, rank:], along[1, cut, rank:]), root))
        weights = base[cut, :] - step_size * fitted
        if last:
            for n, part in enumerate((*halves(weights), *halves(fitted))):
                split[cut, n * columns : (n + 1) * columns] = part
        else:
            base[cut, :] = weights
            start(banded(outgoing, out_sems, k))
            add_up(total, (high, low), halves(weights))

    over_bands(rows, step)
    if last:
        order = order_ref[...]

        def scatter(k):
            cut = band(k)
            positions = lax.broadcasted_iota(jnp.int32, (TILE, rows), 0) + k * TILE
            chosen = jnp.where(positions == order, 1.0, 0.0).astype(bf16)
            parts = jnp.dot(chosen, split[...], preferred_element_type=f32)
            sums[cut, :] = parts[:, :columns] + parts[:, columns : 2 * columns]
            base[cut, :] = parts[:, 2 * columns : 3 * columns] + parts[:, 3 * columns :]
            start(banded(outgoing, out_sems, k))

        over_bands(rows, scatter)
    else:
        sent = send_up(total, leaf, group, leaf_ref, group_ref, end_sems)
        finish(sent)
    over_bands(rows, lambda k: finish(banded(outgoing, out_sems, k)))


def fit(last, sums, base, along, root, order):
    rows, columns = sums.shape
    rank = root.shape[1]
    state = ((rows, columns), f32)
    scratch = [pltpu.VMEM(*state)] * 2 + [pltpu.VMEM(along.shape, bf16)]
    sems = [DMA((4, bands(rows))), DMA((2, bands(rows)))]
    if last:
        outs = [state, state]
        scratch += [pltpu.VMEM((rows, 4 * columns), bf16)]
    else:
        outs = [state, ((rank, columns), f32), ((columns, rank), f32)]
        scratch += [pltpu.VMEM((2 * rank, columns), f32)]
        scratch += [pltpu.VMEM(*out) for out in outs[1:]]
        sems += [DMA((2,))]
    return call(
        functools.partial(fit_kernel, last),
        outs,
        18 * rows * columns * rank,
        sums,
        base,
        along,
        root,
        *((order,) if last else ()),
        in_specs=[HBM] * 3 + [VMEM] * (2 if last else 1),
        near_by=2 if last else 1,
        out_specs=[HBM] * len(outs),
        scratch_shapes=scratch + sems,
    )


def near_kernel(first, *refs):
    old_ref, *refs = refs
    given, refs = refs[: 1 if first else 2], refs[1 if first else 2 :]
    along_ref, *refs = refs
    siblings, refs = refs[:SIDE], refs[SIDE:]
    sum_ref, base_ref, *refs = refs
    if first:
        split_ref, block, *refs = refs
    old, sums, base, leaf, split, ready, *refs = refs
    if not first:
        now, *refs = refs
    in_sems, out_sems, start_sems = refs
    rank = siblings[0].shape[0]
    rows = sums.shape[0]
    outgoing = ((sums, sum_ref), (base, base_ref))
    if first:
        arrived = copies_of((old_ref, old, start_sems.at[0]))
        pairs = ((given[0], block),)
        outgoing += ((split.at[0], split_ref.at[0]), (split.at[1], split_ref.at[1]))
    else:
        arrived = copies_of((given[0], now, start_sems.at[0]))
        pairs = ((given[1].at[0], split.at[0]), (given[1].at[1], split.at[1]), (old_ref, old))
    arrived += copies_of((along_ref.at[:, :, pl.ds(0, rank)], leaf, start_sems.at[1]))
    start(arrived)
    over_bands(rows, lambda k: (start(banded(pairs, in_sems, k)), None)[1])
    total = siblings[0][...]
    for ref in siblings[1:]:
        total = total + ref[...]
    total = halves(total)
    finish(arrived)
    ready[0], ready[1] = halves(step_size * old[...] if first else now[...])

    def step(k):
        cut = band(k)
        finish(banded(pairs, in_sems, k))
        if first:
            split[0, cut, :], split[1, cut, :] = halves(block[cut, :])
        weights = step_size * old[cut, :] if first else now[cut, :]
        near = product((split[0, cut, :], split[1, cut, :]), (ready[0], ready[1]))
        sums[cut, :] = near + product((leaf[0, cut, :], leaf[1, cut, :]), total)
        base[cut, :] = weights - step_size * shrink_rate * weights + step_size * old[cut, :]
        start(banded(outgoing, out_sems, k))

    over_bands(rows, step)
    over_bands(rows, lambda k: finish(banded(outgoing, out_sems, k)))


def near_sum(blocks, weights, targets, along, siblings):
    rows, columns = targets.shape
    rank = siblings[0].shape[0]
    first = weights is None
    state = ((rows, columns), f32)
    split = ((2, rows, rows), bf16)
    shapes = [((rows, rows), f32)] if first else []
    shapes += [state] * 3 + [((2, rows, rank), bf16), split, ((2, rows, columns), bf16)]
    shapes += [] if first else [state]
    return call(
        functools.partial(near_kernel, first),
        [state] * 2 + ([split] if first else []),
        6 * rows * rows * columns,
        targets,
        *(() if first else (weights,)),
        blocks,
        along,
        *siblings,
        in_specs=[HBM] * (3 if first else 4) + [VMEM] * SIDE,
        near_by=SIDE - 1,
        out_specs=[HBM] * (3 if first else 2),
        scratch_shapes=[pltpu.VMEM(*shape) for shape in shapes]
        + [DMA((3, bands(rows))), DMA((4, bands(rows))), DMA((2,))],
    )


def sibling_kernel(split_ref, *refs):
    parts, (first_ref, *out_refs) = refs[:SIDE], refs[SIDE : 2 * SIDE]
    split, sums, in_sem, out_sems = refs[2 * SIDE :]
    rank = parts[0].shape[0]
    arriving = start(copies_of((split_ref, split, in_sem)))
    coefficients = halves(jnp.concatenate([ref[...] for ref in parts]))
    finish(arriving)
    sums[...] = product((split[0], split[1]), coefficients)
    outs = enumerate(out_refs, 1)
    sent = start(
        copies_of(*((sums.at[pl.ds(k * rank, rank)], out, out_sems.at[k - 1]) for k, out in outs))
    )
    first_ref[...] = sums[:rank, :]
    finish(sent)


def sibling_sums(couplings, parts):
    rank, columns = parts[0].shape
    return call(
        sibling_kernel,
        [((rank, columns), f32)] * SIDE,
        6 * SIDE * SIDE * rank * rank * columns,
        couplings,
        *parts,
        in_specs=[HBM] + [VMEM] * SIDE,
        near_by=SIDE - 1,
        out_specs=[VMEM] + [HBM] * (SIDE - 1),
        scratch_shapes=[
            pltpu.VMEM(couplings.shape, bf16),
            pltpu.VMEM((SIDE * rank, columns), f32),
            DMA(()),
            DMA((SIDE - 1,)),
        ],
    )


def sum_kernel(parts_ref, out_ref):
    total = parts_ref[0]
    for k in range(1, parts_ref.shape[0]):
        total = total + parts_ref[k]
    for k in range(out_ref.shape[0]):
        out_ref[k] = total
    out_ref[lax.axis_index("grp")] = jnp.zeros_like(total)


def sum_copies(parts):
    length = lax.axis_size("grp")
    return call(sum_kernel, [((length, *parts.shape[1:]), f32)], 0, parts, near_by=1)[0]


def root_kernel(split_ref, parts_ref, out_ref):
    groups, _, rank = parts_ref.shape
    parts = jnp.concatenate([parts_ref[k] for k in range(groups)], axis=1)
    couplings = [split_ref[k].reshape(groups * rank, rank) for k in range(2)]
    root = product(halves(parts), couplings)
    for k in range(out_ref.shape[0]):
        out_ref[k] = root


def root_copies(parts, tops):
    groups, share, rank = parts.shape
    outs = [((lax.axis_size("sib"), share, rank), f32)]
    return call(root_kernel, outs, 6 * groups * share * rank * rank, tops, parts, near_by=1)[0]


def shards(targets, leaf_order, near_block, leaf_basis, sibling_coupling, transfer, top_coupling):
    ordering = leaf_order[0]
    _, columns = targets.shape
    rank = transfer.shape[0]
    sibs = lax.axis_size("sib")
    share = columns // sibs
    tree_targets = targets.at[ordering].get(unique_indices=True, mode="promise_in_bounds")
    along, leaf_part, group_part = begin(tree_targets, leaf_basis, transfer)
    own, *sent = arrange(sibling_coupling, top_coupling)
    got = [shifted(block, ahead, 0) for ahead, block in enumerate(sent, 1)]
    row_couplings, top_blocks = couple(top_coupling, own, got)
    blocks = near_block
    weights = None
    for iteration in range(ITERS):
        last = iteration == ITERS - 1
        arrived = exchange(group_part.reshape(sibs, share, rank), "sib")
        parts = [leaf_part] + [shifted(leaf_part, 0, behind) for behind in range(1, SIDE)]
        if iteration == 0:
            tops = [top_blocks] + [shifted(top_blocks, 0, behind) for behind in range(1, SIDE)]
            tops = place(tops)
        group_copies = sum_copies(arrived)
        others = exchange(group_copies, "grp")
        sums = sibling_sums(row_couplings, parts)
        sums = [sums[0]] + [shifted(sums[ahead], -ahead, 0) for ahead in range(1, SIDE)]
        roots = root_copies(others, tops)
        root_whole = exchange(roots, "sib").reshape(columns, rank)
        near, base, *split = near_sum(blocks, weights, tree_targets, along, sums)
        blocks = split[0] if split else blocks
        outs = fit(last, near, base, along, root_whole, leaf_order)
        if not last:
            weights, leaf_part, group_part = outs
    return tuple(outs)


def solution(mesh):
    split = P(("grp", "sib"), None)
    return jax.shard_map(
        shards,
        mesh=mesh,
        in_specs=(split,) * 6 + (P("grp", "sib"),),
        out_specs=(split, split),
        check_vma=False,
    )
```

profile of v0, /device:TPU:1, one launch (start us, length us, event | category | flops | bytes accessed | tf_op | source)
XLA Modules:
  0.0 188.7 jit_solution(9669607352008658367)
XLA Ops:
  0.6 2.5 %shard_map.87 = (f32[128,512]{1,0:T(8,128)}, f32[128,640]{1,0:T(8,128)}, f32[128,640]{1,0:T(8,128)}, f32[128,640]{1,0:T(8,128)}) custom-call(f32[128,2048]{1,0:T(8,128)} %row_ref.1, f32[128,128]{1,0:T(8,128)} %top_ref.3), custom_call_target="tpu_custom_call" | custom-call | bytes 2359296 | tf_op jit(solution)/shard_map/pallas_call | solution.py:38
  5.3 2.6 %collective-permute-start.1 = (f32[128,640]{1,0:T(8,128)}, f32[128,640]{1,0:T(8,128)S(1)}, u32[]{:S(2)}, u32[]{:S(2)}) collective-permute-start(f32[128,640]{1,0:T(8,128)} %get-tuple-element.39), channel_id=1, source_target_pairs={{0,8},{1,9},{2,10},{3,11},{4,12},{5,13},{6,14},{7,15},{8,0},{9,1},... | collective-permute-start | bytes 983048 | tf_op jit(solution)/shard_map/ppermute | solution.py:57
  9.7 4.1 %gather_fusion = f32[1280,256]{1,0:T(8,128)} fusion(f32[1280,256]{1,0:T(8,128)S(1)} %copy-done, s32[2048]{0:T(1024)S(1)} %pad_clamp_fusion), kind=kCustom, calls=%fused_computation | custom fusion | bytes 2626560 | tf_op jit(solution)/shard_map/gather | solution.py:449
  13.8 4.5 %shard_map.86 = (bf16[2,1280,256]{2,1,0:T(8,128)(2,1)}, f32[128,256]{1,0:T(8,128)}, f32[256,128]{1,0:T(8,128)}) custom-call(f32[1280,256]{1,0:T(8,128)} %gather_fusion, f32[1280,128]{1,0:T(8,128)} %basis_ref.1, f32[128,128]{1,0:T(8,128)S(1)} %copy-done.2), custom_call_target="tpu_custom_call" | custom-call | flops 754974720 | bytes 3604480 | tf_op jit(solution)/shard_map/pallas_call | solution.py:38
  18.4 2.6 %collective-permute-start.5 = (f32[128,256]{1,0:T(8,128)}, f32[128,256]{1,0:T(8,128)S(1)}, u32[]{:S(2)}, u32[]{:S(2)}) collective-permute-start(f32[128,256]{1,0:T(8,128)} %get-tuple-element.42.refs_0_), channel_id=1, source_target_pairs={{0,3},{1,0},{2,1},{3,2},{4,7},{5,4},{6,5},{7,6},{8,11},{9,8},{10,9... | collective-permute-start | bytes 393224 | tf_op jit(solution)/shard_map/ppermute | solution.py:57
  24.4 2.5 %collective-permute-start.11 = (f32[4,128,128]{2,1,0:T(8,128)}, f32[4,128,128]{2,1,0:T(8,128)S(1)}, u32[]{:S(2)}, u32[]{:S(2)}) collective-permute-start(f32[4,128,128]{2,1,0:T(8,128)} %get-tuple-element.49.refs_0_), channel_id=1, source_target_pairs={{0,3},{1,0},{2,1},{3,2},{4,7},{5,4},{6,5},{7,6},{8,11},{9,8},{10,9... | collective-permute-start | bytes 786440 | tf_op jit(solution)/shard_map/ppermute | solution.py:57
  26.9 4.5 %all-to-all-start = ((f32[16,16,128]{2,1,0:T(8,128)}), f32[16,16,128]{2,1,0:T(8,128)S(1)}, u32[]{:S(2)}, u32[]{:S(2)}) async-start(f32[16,16,128]{2,1,0:T(8,128)} %bitcast.1), calls=%async_computation | async-start | bytes 262144 | tf_op jit(solution)/shard_map/all_to_all | solution.py:48
  31.4 3.0 %collective-permute-start.4 = (f32[128,256]{1,0:T(8,128)S(1)}, f32[128,256]{1,0:T(8,128)S(1)}, u32[]{:S(2)}, u32[]{:S(2)}) collective-permute-start(f32[128,256]{1,0:T(8,128)S(1)} %copy-done.3), channel_id=1, source_target_pairs={{0,2},{1,3},{2,0},{3,1},{4,6},{5,7},{6,4},{7,5},{8,10},{9,11},{10,... | collective-permute-start | bytes 393224 | tf_op jit(solution)/shard_map/ppermute | solution.py:57
  38.9 11.9 %all-to-all-start.1 = ((f32[16,16,128]{2,1,0:T(8,128)}), f32[16,16,128]{2,1,0:T(8,128)S(1)}, u32[]{:S(2)}, u32[]{:S(2)}) async-start(f32[16,16,128]{2,1,0:T(8,128)} %shard_map.92), calls=%async_computation.1 | async-start | bytes 262144 | tf_op jit(solution)/shard_map/all_to_all | solution.py:48
  50.8 4.2 %shard_map.89 = (f32[128,256]{1,0:T(8,128)}, f32[128,256]{1,0:T(8,128)}, f32[128,256]{1,0:T(8,128)}, f32[128,256]{1,0:T(8,128)}) custom-call(bf16[2,512,512]{2,1,0:T(8,128)(2,1)} %get-tuple-element.41.split_ref, f32[128,256]{1,0:T(8,128)} %get-tuple-element.42.refs_0_, f32[128,256]{1,0:T(8,128)S(1)} %collective-permute-done.3.refs_1_, ...), custom_call_target="tpu_custom_call" | custom-call | flops 402653184 | bytes 2097152 | tf_op jit(solution)/shard_map/pallas_call | solution.py:38
  57.6 2.3 %shard_map.91.split_ref = bf16[2,16,128,128]{3,2,1,0:T(8,128)(2,1)} custom-call(f32[4,128,128]{2,1,0:T(8,128)} %get-tuple-element.49.refs_0_, f32[4,128,128]{2,1,0:T(8,128)S(1)} %collective-permute-done.9.refs_1_, f32[4,128,128]{2,1,0:T(8,128)S(1)} %collective-permute-done.10.refs_2_, f32[4,128,128]{2,1,0:T(8,128)S(1)} %collective-permute-done.11.refs_3_), custom_call_target="tpu_custom_call" | custom-call | bytes 2097152 | tf_op jit(solution)/shard_map/pallas_call | solution.py:38
  62.1 5.1 %all-to-all-start.2 = ((f32[16,16,128]{2,1,0:T(8,128)}), f32[16,16,128]{2,1,0:T(8,128)S(1)}, u32[]{:S(2)}, u32[]{:S(2)}) async-start(f32[16,16,128]{2,1,0:T(8,128)} %shard_map.93), calls=%async_computation.2 | async-start | bytes 262144 | tf_op jit(solution)/shard_map/all_to_all | solution.py:48
  67.3 8.3 %shard_map.90 = (f32[1280,256]{1,0:T(8,128)}, f32[1280,256]{1,0:T(8,128)}, bf16[2,1280,1280]{2,1,0:T(8,128)(2,1)}) custom-call(f32[1280,256]{1,0:T(8,128)} %gather_fusion, f32[1280,1280]{1,0:T(8,128)} %refs_1_.1, bf16[2,1280,256]{2,1,0:T(8,128)(2,1)} %get-tuple-element.36.refs_2_.refs_3_, f32[128,256]{1,0:T(8,128)} %get-tuple-element.43.refs_3_, ...), custom_call_target="tpu_custom_call" | custom-call | flops 2516582400 | bytes 18874368 | tf_op jit(solution)/shard_map/pallas_call | solution.py:38
  75.6 5.5 %shard_map.94 = (f32[1280,256]{1,0:T(8,128)}, f32[128,256]{1,0:T(8,128)}, f32[256,128]{1,0:T(8,128)}) custom-call(f32[1280,256]{1,0:T(8,128)} %get-tuple-element.47.refs_0_, f32[1280,256]{1,0:T(8,128)} %get-tuple-element.48.refs_1_, bf16[2,1280,256]{2,1,0:T(8,128)(2,1)} %get-tuple-element.36.refs_2_.refs_3_, f32[256,128]{1,0:T(8,128)S(1)} %bitcast.9), custom_call_target="tpu_custom_call" | custom-call | flops 754974720 | bytes 5636096 | tf_op jit(solution)/shard_map/pallas_call | solution.py:38
  81.1 6.7 %all-to-all-start.3 = ((f32[16,16,128]{2,1,0:T(8,128)}), f32[16,16,128]{2,1,0:T(8,128)S(1)}, u32[]{:S(2)}, u32[]{:S(2)}) async-start(f32[16,16,128]{2,1,0:T(8,128)} %bitcast.11), calls=%async_computation.3 | async-start | bytes 262144 | tf_op jit(solution)/shard_map/all_to_all | solution.py:48
  87.8 2.6 %collective-permute-start.14 = (f32[128,256]{1,0:T(8,128)}, f32[128,256]{1,0:T(8,128)S(1)}, u32[]{:S(2)}, u32[]{:S(2)}) collective-permute-start(f32[128,256]{1,0:T(8,128)} %get-tuple-element.53.refs_0_), channel_id=1, source_target_pairs={{0,3},{1,0},{2,1},{3,2},{4,7},{5,4},{6,5},{7,6},{8,11},{9,8},{10,9... | collective-permute-start | bytes 393224 | tf_op jit(solution)/shard_map/ppermute | solution.py:57
  91.5 3.1 %all-to-all-done.3.parts_ref = f32[16,16,128]{2,1,0:T(8,128)S(1)} async-done(((f32[16,16,128]{2,1,0:T(8,128)}), f32[16,16,128]{2,1,0:T(8,128)S(1)}, u32[]{:S(2)}, u32[]{:S(2)}) %all-to-all-start.3) | async-done | bytes 131104 | tf_op jit(solution)/shard_map/all_to_all | solution.py:48
  95.3 10.6 %all-to-all-start.4 = ((f32[16,16,128]{2,1,0:T(8,128)}), f32[16,16,128]{2,1,0:T(8,128)S(1)}, u32[]{:S(2)}, u32[]{:S(2)}) async-start(f32[16,16,128]{2,1,0:T(8,128)} %shard_map.97), calls=%async_computation.4 | async-start | bytes 262144 | tf_op jit(solution)/shard_map/all_to_all | solution.py:48
  106.0 4.1 %shard_map.95 = (f32[128,256]{1,0:T(8,128)}, f32[128,256]{1,0:T(8,128)}, f32[128,256]{1,0:T(8,128)}, f32[128,256]{1,0:T(8,128)}) custom-call(bf16[2,512,512]{2,1,0:T(8,128)(2,1)} %get-tuple-element.41.split_ref, f32[128,256]{1,0:T(8,128)} %get-tuple-element.53.refs_0_, f32[128,256]{1,0:T(8,128)S(1)} %collective-permute-done.12.refs_1_, ...), custom_call_target="tpu_custom_call" | custom-call | flops 402653184 | bytes 2097152 | tf_op jit(solution)/shard_map/pallas_call | solution.py:38
  111.6 3.2 %all-to-all-done.4.parts_ref = f32[16,16,128]{2,1,0:T(8,128)S(1)} async-done(((f32[16,16,128]{2,1,0:T(8,128)}), f32[16,16,128]{2,1,0:T(8,128)S(1)}, u32[]{:S(2)}, u32[]{:S(2)}) %all-to-all-start.4) | async-done | bytes 131104 | tf_op jit(solution)/shard_map/all_to_all | solution.py:48
  117.0 3.5 %all-to-all-start.5 = ((f32[16,16,128]{2,1,0:T(8,128)}), f32[16,16,128]{2,1,0:T(8,128)S(1)}, u32[]{:S(2)}, u32[]{:S(2)}) async-start(f32[16,16,128]{2,1,0:T(8,128)} %shard_map.98), calls=%async_computation.5 | async-start | bytes 262144 | tf_op jit(solution)/shard_map/all_to_all | solution.py:48
  120.7 7.9 %shard_map.96 = (f32[1280,256]{1,0:T(8,128)}, f32[1280,256]{1,0:T(8,128)}) custom-call(f32[1280,256]{1,0:T(8,128)} %gather_fusion, f32[1280,256]{1,0:T(8,128)} %get-tuple-element.51.refs_1_, bf16[2,1280,1280]{2,1,0:T(8,128)(2,1)} %get-tuple-element.52.refs_2_, bf16[2,1280,256]{2,1,0:T(8,128)(2,1)} %get-tuple-element.36.refs_2_.refs_3_, ...), custom_call_target="tpu_custom_call" | custom-call | flops 2516582400 | bytes 13631488 | tf_op jit(solution)/shard_map/pallas_call | solution.py:38
  128.6 5.5 %shard_map.99 = (f32[1280,256]{1,0:T(8,128)}, f32[128,256]{1,0:T(8,128)}, f32[256,128]{1,0:T(8,128)}) custom-call(f32[1280,256]{1,0:T(8,128)} %get-tuple-element.58.refs_0_, f32[1280,256]{1,0:T(8,128)} %get-tuple-element.59.refs_1_, bf16[2,1280,256]{2,1,0:T(8,128)(2,1)} %get-tuple-element.36.refs_2_.refs_3_, f32[256,128]{1,0:T(8,128)S(1)} %bitcast.8), custom_call_target="tpu_custom_call" | custom-call | flops 754974720 | bytes 5636096 | tf_op jit(solution)/shard_map/pallas_call | solution.py:38
  134.1 6.5 %all-to-all-start.6 = ((f32[16,16,128]{2,1,0:T(8,128)}), f32[16,16,128]{2,1,0:T(8,128)S(1)}, u32[]{:S(2)}, u32[]{:S(2)}) async-start(f32[16,16,128]{2,1,0:T(8,128)} %bitcast.12), calls=%async_computation.6 | async-start | bytes 262144 | tf_op jit(solution)/shard_map/all_to_all | solution.py:48
  140.6 2.6 %collective-permute-start.20 = (f32[128,256]{1,0:T(8,128)}, f32[128,256]{1,0:T(8,128)S(1)}, u32[]{:S(2)}, u32[]{:S(2)}) collective-permute-start(f32[128,256]{1,0:T(8,128)} %get-tuple-element.62.refs_0_), channel_id=1, source_target_pairs={{0,3},{1,0},{2,1},{3,2},{4,7},{5,4},{6,5},{7,6},{8,11},{9,8},{10,9... | collective-permute-start | bytes 393224 | tf_op jit(solution)/shard_map/ppermute | solution.py:57
  144.3 3.2 %all-to-all-done.6.parts_ref = f32[16,16,128]{2,1,0:T(8,128)S(1)} async-done(((f32[16,16,128]{2,1,0:T(8,128)}), f32[16,16,128]{2,1,0:T(8,128)S(1)}, u32[]{:S(2)}, u32[]{:S(2)}) %all-to-all-start.6) | async-done | bytes 131104 | tf_op jit(solution)/shard_map/all_to_all | solution.py:48
  148.2 9.4 %all-to-all-start.7 = ((f32[16,16,128]{2,1,0:T(8,128)}), f32[16,16,128]{2,1,0:T(8,128)S(1)}, u32[]{:S(2)}, u32[]{:S(2)}) async-start(f32[16,16,128]{2,1,0:T(8,128)} %shard_map.102), calls=%async_computation.7 | async-start | bytes 262144 | tf_op jit(solution)/shard_map/all_to_all | solution.py:48
  157.6 4.1 %shard_map.100 = (f32[128,256]{1,0:T(8,128)}, f32[128,256]{1,0:T(8,128)}, f32[128,256]{1,0:T(8,128)}, f32[128,256]{1,0:T(8,128)}) custom-call(bf16[2,512,512]{2,1,0:T(8,128)(2,1)} %get-tuple-element.41.split_ref, f32[128,256]{1,0:T(8,128)} %get-tuple-element.62.refs_0_, f32[128,256]{1,0:T(8,128)S(1)} %collective-permute-done.18.refs_1_, ...), custom_call_target="tpu_custom_call" | custom-call | flops 402653184 | bytes 2097152 | tf_op jit(solution)/shard_map/pallas_call | solution.py:38
  163.6 2.9 %all-to-all-done.7.parts_ref = f32[16,16,128]{2,1,0:T(8,128)S(1)} async-done(((f32[16,16,128]{2,1,0:T(8,128)}), f32[16,16,128]{2,1,0:T(8,128)S(1)}, u32[]{:S(2)}, u32[]{:S(2)}) %all-to-all-start.7) | async-done | bytes 131104 | tf_op jit(solution)/shard_map/all_to_all | solution.py:48
  168.7 3.5 %all-to-all-start.8 = ((f32[16,16,128]{2,1,0:T(8,128)}), f32[16,16,128]{2,1,0:T(8,128)S(1)}, u32[]{:S(2)}, u32[]{:S(2)}) async-start(f32[16,16,128]{2,1,0:T(8,128)} %shard_map.103), calls=%async_computation.8 | async-start | bytes 262144 | tf_op jit(solution)/shard_map/all_to_all | solution.py:48
  172.6 7.9 %shard_map.101 = (f32[1280,256]{1,0:T(8,128)}, f32[1280,256]{1,0:T(8,128)}) custom-call(f32[1280,256]{1,0:T(8,128)} %gather_fusion, f32[1280,256]{1,0:T(8,128)} %get-tuple-element.61.refs_1_, bf16[2,1280,1280]{2,1,0:T(8,128)(2,1)} %get-tuple-element.52.refs_2_, bf16[2,1280,256]{2,1,0:T(8,128)(2,1)} %get-tuple-element.36.refs_2_.refs_3_, ...), custom_call_target="tpu_custom_call" | custom-call | flops 2516582400 | bytes 13631488 | tf_op jit(solution)/shard_map/pallas_call | solution.py:38
  180.5 7.9 %shard_map.104 = (f32[1280,256]{1,0:T(8,128)}, f32[1280,256]{1,0:T(8,128)}) custom-call(f32[1280,256]{1,0:T(8,128)} %get-tuple-element.67.refs_0_, f32[1280,256]{1,0:T(8,128)} %get-tuple-element.68.refs_1_, bf16[2,1280,256]{2,1,0:T(8,128)(2,1)} %get-tuple-element.36.refs_2_.refs_3_, f32[256,128]{1,0:T(8,128)S(1)} %bitcast.10, s32[1,1280]{1,0:T(1,128)S(1)} %copy-done.1), custom_call_target="tpu_custom_call" | custom-call | flops 754974720 | bytes 6689792 | tf_op jit(solution)/shard_map/pallas_call | solution.py:38
  (64 shorter events, 28.7 us)
Async XLA Ops:
  3.2 17.7 %collective-permute-start = (f32[128,640]{1,0:T(8,128)}, f32[128,640]{1,0:T(8,128)S(1)}, u32[]{:S(2)}, u32[]{:S(2)}) collective-permute-start(f32[128,640]{1,0:T(8,128)} %get-tuple-element.38), channel_id=1, source_target_pairs={{0,4},{1,5},{2,6},{3,7},{4,8},{5,9},{6,10},{7,11},{8,12},{9,13},{1... | collective-permute-start | bytes 983048 | tf_op jit(solution)/shard_map/ppermute | solution.py:57
  5.3 17.0 %collective-permute-start.1 = (f32[128,640]{1,0:T(8,128)}, f32[128,640]{1,0:T(8,128)S(1)}, u32[]{:S(2)}, u32[]{:S(2)}) collective-permute-start(f32[128,640]{1,0:T(8,128)} %get-tuple-element.39), channel_id=1, source_target_pairs={{0,8},{1,9},{2,10},{3,11},{4,12},{5,13},{6,14},{7,15},{8,0},{9,1},... | collective-permute-start | bytes 983048 | tf_op jit(solution)/shard_map/ppermute | solution.py:57
  7.9 14.4 %collective-permute-start.2 = (f32[128,640]{1,0:T(8,128)}, f32[128,640]{1,0:T(8,128)S(1)}, u32[]{:S(2)}, u32[]{:S(2)}) collective-permute-start(f32[128,640]{1,0:T(8,128)} %get-tuple-element.40), channel_id=1, source_target_pairs={{0,12},{1,13},{2,14},{3,15},{4,0},{5,1},{6,2},{7,3},{8,4},{9,5},{1... | collective-permute-start | bytes 983048 | tf_op jit(solution)/shard_map/ppermute | solution.py:57
  18.4 18.0 %collective-permute-start.5 = (f32[128,256]{1,0:T(8,128)}, f32[128,256]{1,0:T(8,128)S(1)}, u32[]{:S(2)}, u32[]{:S(2)}) collective-permute-start(f32[128,256]{1,0:T(8,128)} %get-tuple-element.42.refs_0_), channel_id=1, source_target_pairs={{0,3},{1,0},{2,1},{3,2},{4,7},{5,4},{6,5},{7,6},{8,11},{9,8},{10,9... | collective-permute-start | bytes 393224 | tf_op jit(solution)/shard_map/ppermute | solution.py:57
  24.4 32.6 %collective-permute-start.11 = (f32[4,128,128]{2,1,0:T(8,128)}, f32[4,128,128]{2,1,0:T(8,128)S(1)}, u32[]{:S(2)}, u32[]{:S(2)}) collective-permute-start(f32[4,128,128]{2,1,0:T(8,128)} %get-tuple-element.49.refs_0_), channel_id=1, source_target_pairs={{0,3},{1,0},{2,1},{3,2},{4,7},{5,4},{6,5},{7,6},{8,11},{9,8},{10,9... | collective-permute-start | bytes 786440 | tf_op jit(solution)/shard_map/ppermute | solution.py:57
  26.9 11.3 %all-to-all-start = ((f32[16,16,128]{2,1,0:T(8,128)}), f32[16,16,128]{2,1,0:T(8,128)S(1)}, u32[]{:S(2)}, u32[]{:S(2)}) async-start(f32[16,16,128]{2,1,0:T(8,128)} %bitcast.1), calls=%async_computation | async-start | bytes 262144 | tf_op jit(solution)/shard_map/all_to_all | solution.py:48
  31.4 19.4 %collective-permute-start.4 = (f32[128,256]{1,0:T(8,128)S(1)}, f32[128,256]{1,0:T(8,128)S(1)}, u32[]{:S(2)}, u32[]{:S(2)}) collective-permute-start(f32[128,256]{1,0:T(8,128)S(1)} %copy-done.3), channel_id=1, source_target_pairs={{0,2},{1,3},{2,0},{3,1},{4,6},{5,7},{6,4},{7,5},{8,10},{9,11},{10,... | collective-permute-start | bytes 393224 | tf_op jit(solution)/shard_map/ppermute | solution.py:57
  34.3 16.5 %collective-permute-start.3 = (f32[128,256]{1,0:T(8,128)S(1)}, f32[128,256]{1,0:T(8,128)S(1)}, u32[]{:S(2)}, u32[]{:S(2)}) collective-permute-start(f32[128,256]{1,0:T(8,128)S(1)} %copy-done.3), channel_id=1, source_target_pairs={{0,1},{1,2},{2,3},{3,0},{4,5},{5,6},{6,7},{7,4},{8,9},{9,10},{10,1... | collective-permute-start | bytes 393224 | tf_op jit(solution)/shard_map/ppermute | solution.py:57
  34.6 23.0 %collective-permute-start.10 = (f32[4,128,128]{2,1,0:T(8,128)}, f32[4,128,128]{2,1,0:T(8,128)S(1)}, u32[]{:S(2)}, u32[]{:S(2)}) collective-permute-start(f32[4,128,128]{2,1,0:T(8,128)} %get-tuple-element.49.refs_0_), channel_id=1, source_target_pairs={{0,2},{1,3},{2,0},{3,1},{4,6},{5,7},{6,4},{7,5},{8,10},{9,11},{10,... | collective-permute-start | bytes 786440 | tf_op jit(solution)/shard_map/ppermute | solution.py:57
  36.4 21.2 %collective-permute-start.9 = (f32[4,128,128]{2,1,0:T(8,128)}, f32[4,128,128]{2,1,0:T(8,128)S(1)}, u32[]{:S(2)}, u32[]{:S(2)}) collective-permute-start(f32[4,128,128]{2,1,0:T(8,128)} %get-tuple-element.49.refs_0_), channel_id=1, source_target_pairs={{0,1},{1,2},{2,3},{3,0},{4,5},{5,6},{6,7},{7,4},{8,9},{9,10},{10,1... | collective-permute-start | bytes 786440 | tf_op jit(solution)/shard_map/ppermute | solution.py:57
  38.9 21.1 %all-to-all-start.1 = ((f32[16,16,128]{2,1,0:T(8,128)}), f32[16,16,128]{2,1,0:T(8,128)S(1)}, u32[]{:S(2)}, u32[]{:S(2)}) async-start(f32[16,16,128]{2,1,0:T(8,128)} %shard_map.92), calls=%async_computation.1 | async-start | bytes 262144 | tf_op jit(solution)/shard_map/all_to_all | solution.py:48
  55.0 12.3 %collective-permute-start.6 = (f32[128,256]{1,0:T(8,128)}, f32[128,256]{1,0:T(8,128)S(1)}, u32[]{:S(2)}, u32[]{:S(2)}) collective-permute-start(f32[128,256]{1,0:T(8,128)} %get-tuple-element.44), channel_id=1, source_target_pairs={{0,12},{1,13},{2,14},{3,15},{4,0},{5,1},{6,2},{7,3},{8,4},{9,5},{1... | collective-permute-start | bytes 393224 | tf_op jit(solution)/shard_map/ppermute | solution.py:57
  56.4 10.9 %collective-permute-start.7 = (f32[128,256]{1,0:T(8,128)}, f32[128,256]{1,0:T(8,128)S(1)}, u32[]{:S(2)}, u32[]{:S(2)}) collective-permute-start(f32[128,256]{1,0:T(8,128)} %get-tuple-element.45), channel_id=1, source_target_pairs={{0,8},{1,9},{2,10},{3,11},{4,12},{5,13},{6,14},{7,15},{8,0},{9,1},... | collective-permute-start | bytes 393224 | tf_op jit(solution)/shard_map/ppermute | solution.py:57
  57.0 10.3 %collective-permute-start.8 = (f32[128,256]{1,0:T(8,128)}, f32[128,256]{1,0:T(8,128)S(1)}, u32[]{:S(2)}, u32[]{:S(2)}) collective-permute-start(f32[128,256]{1,0:T(8,128)} %get-tuple-element.46), channel_id=1, source_target_pairs={{0,4},{1,5},{2,6},{3,7},{4,8},{5,9},{6,10},{7,11},{8,12},{9,13},{1... | collective-permute-start | bytes 393224 | tf_op jit(solution)/shard_map/ppermute | solution.py:57
  62.1 13.5 %all-to-all-start.2 = ((f32[16,16,128]{2,1,0:T(8,128)}), f32[16,16,128]{2,1,0:T(8,128)S(1)}, u32[]{:S(2)}, u32[]{:S(2)}) async-start(f32[16,16,128]{2,1,0:T(8,128)} %shard_map.93), calls=%async_computation.2 | async-start | bytes 262144 | tf_op jit(solution)/shard_map/all_to_all | solution.py:48
  81.1 13.5 %all-to-all-start.3 = ((f32[16,16,128]{2,1,0:T(8,128)}), f32[16,16,128]{2,1,0:T(8,128)S(1)}, u32[]{:S(2)}, u32[]{:S(2)}) async-start(f32[16,16,128]{2,1,0:T(8,128)} %bitcast.11), calls=%async_computation.3 | async-start | bytes 262144 | tf_op jit(solution)/shard_map/all_to_all | solution.py:48
  87.8 18.1 %collective-permute-start.14 = (f32[128,256]{1,0:T(8,128)}, f32[128,256]{1,0:T(8,128)S(1)}, u32[]{:S(2)}, u32[]{:S(2)}) collective-permute-start(f32[128,256]{1,0:T(8,128)} %get-tuple-element.53.refs_0_), channel_id=1, source_target_pairs={{0,3},{1,0},{2,1},{3,2},{4,7},{5,4},{6,5},{7,6},{8,11},{9,8},{10,9... | collective-permute-start | bytes 393224 | tf_op jit(solution)/shard_map/ppermute | solution.py:57
  90.4 15.6 %collective-permute-start.13 = (f32[128,256]{1,0:T(8,128)}, f32[128,256]{1,0:T(8,128)S(1)}, u32[]{:S(2)}, u32[]{:S(2)}) collective-permute-start(f32[128,256]{1,0:T(8,128)} %get-tuple-element.53.refs_0_), channel_id=1, source_target_pairs={{0,2},{1,3},{2,0},{3,1},{4,6},{5,7},{6,4},{7,5},{8,10},{9,11},{10,... | collective-permute-start | bytes 393224 | tf_op jit(solution)/shard_map/ppermute | solution.py:57
  91.0 15.0 %collective-permute-start.12 = (f32[128,256]{1,0:T(8,128)}, f32[128,256]{1,0:T(8,128)S(1)}, u32[]{:S(2)}, u32[]{:S(2)}) collective-permute-start(f32[128,256]{1,0:T(8,128)} %get-tuple-element.53.refs_0_), channel_id=1, source_target_pairs={{0,1},{1,2},{2,3},{3,0},{4,5},{5,6},{6,7},{7,4},{8,9},{9,10},{10,1... | collective-permute-start | bytes 393224 | tf_op jit(solution)/shard_map/ppermute | solution.py:57
  95.3 19.5 %all-to-all-start.4 = ((f32[16,16,128]{2,1,0:T(8,128)}), f32[16,16,128]{2,1,0:T(8,128)S(1)}, u32[]{:S(2)}, u32[]{:S(2)}) async-start(f32[16,16,128]{2,1,0:T(8,128)} %shard_map.97), calls=%async_computation.4 | async-start | bytes 262144 | tf_op jit(solution)/shard_map/all_to_all | solution.py:48
  110.1 10.5 %collective-permute-start.15 = (f32[128,256]{1,0:T(8,128)}, f32[128,256]{1,0:T(8,128)S(1)}, u32[]{:S(2)}, u32[]{:S(2)}) collective-permute-start(f32[128,256]{1,0:T(8,128)} %get-tuple-element.55), channel_id=1, source_target_pairs={{0,12},{1,13},{2,14},{3,15},{4,0},{5,1},{6,2},{7,3},{8,4},{9,5},{1... | collective-permute-start | bytes 393224 | tf_op jit(solution)/shard_map/ppermute | solution.py:57
  110.7 9.8 %collective-permute-start.16 = (f32[128,256]{1,0:T(8,128)}, f32[128,256]{1,0:T(8,128)S(1)}, u32[]{:S(2)}, u32[]{:S(2)}) collective-permute-start(f32[128,256]{1,0:T(8,128)} %get-tuple-element.56), channel_id=1, source_target_pairs={{0,8},{1,9},{2,10},{3,11},{4,12},{5,13},{6,14},{7,15},{8,0},{9,1},... | collective-permute-start | bytes 393224 | tf_op jit(solution)/shard_map/ppermute | solution.py:57
  111.4 9.3 %collective-permute-start.17 = (f32[128,256]{1,0:T(8,128)}, f32[128,256]{1,0:T(8,128)S(1)}, u32[]{:S(2)}, u32[]{:S(2)}) collective-permute-start(f32[128,256]{1,0:T(8,128)} %get-tuple-element.57), channel_id=1, source_target_pairs={{0,4},{1,5},{2,6},{3,7},{4,8},{5,9},{6,10},{7,11},{8,12},{9,13},{1... | collective-permute-start | bytes 393224 | tf_op jit(solution)/shard_map/ppermute | solution.py:57
  117.0 11.6 %all-to-all-start.5 = ((f32[16,16,128]{2,1,0:T(8,128)}), f32[16,16,128]{2,1,0:T(8,128)S(1)}, u32[]{:S(2)}, u32[]{:S(2)}) async-start(f32[16,16,128]{2,1,0:T(8,128)} %shard_map.98), calls=%async_computation.5 | async-start | bytes 262144 | tf_op jit(solution)/shard_map/all_to_all | solution.py:48
  134.1 13.4 %all-to-all-start.6 = ((f32[16,16,128]{2,1,0:T(8,128)}), f32[16,16,128]{2,1,0:T(8,128)S(1)}, u32[]{:S(2)}, u32[]{:S(2)}) async-start(f32[16,16,128]{2,1,0:T(8,128)} %bitcast.12), calls=%async_computation.6 | async-start | bytes 262144 | tf_op jit(solution)/shard_map/all_to_all | solution.py:48
  140.6 17.0 %collective-permute-start.20 = (f32[128,256]{1,0:T(8,128)}, f32[128,256]{1,0:T(8,128)S(1)}, u32[]{:S(2)}, u32[]{:S(2)}) collective-permute-start(f32[128,256]{1,0:T(8,128)} %get-tuple-element.62.refs_0_), channel_id=1, source_target_pairs={{0,3},{1,0},{2,1},{3,2},{4,7},{5,4},{6,5},{7,6},{8,11},{9,8},{10,9... | collective-permute-start | bytes 393224 | tf_op jit(solution)/shard_map/ppermute | solution.py:57
  143.2 14.4 %collective-permute-start.19 = (f32[128,256]{1,0:T(8,128)}, f32[128,256]{1,0:T(8,128)S(1)}, u32[]{:S(2)}, u32[]{:S(2)}) collective-permute-start(f32[128,256]{1,0:T(8,128)} %get-tuple-element.62.refs_0_), channel_id=1, source_target_pairs={{0,2},{1,3},{2,0},{3,1},{4,6},{5,7},{6,4},{7,5},{8,10},{9,11},{10,... | collective-permute-start | bytes 393224 | tf_op jit(solution)/shard_map/ppermute | solution.py:57
  143.8 13.9 %collective-permute-start.18 = (f32[128,256]{1,0:T(8,128)}, f32[128,256]{1,0:T(8,128)S(1)}, u32[]{:S(2)}, u32[]{:S(2)}) collective-permute-start(f32[128,256]{1,0:T(8,128)} %get-tuple-element.62.refs_0_), channel_id=1, source_target_pairs={{0,1},{1,2},{2,3},{3,0},{4,5},{5,6},{6,7},{7,4},{8,9},{9,10},{10,1... | collective-permute-start | bytes 393224 | tf_op jit(solution)/shard_map/ppermute | solution.py:57
  148.2 18.3 %all-to-all-start.7 = ((f32[16,16,128]{2,1,0:T(8,128)}), f32[16,16,128]{2,1,0:T(8,128)S(1)}, u32[]{:S(2)}, u32[]{:S(2)}) async-start(f32[16,16,128]{2,1,0:T(8,128)} %shard_map.102), calls=%async_computation.7 | async-start | bytes 262144 | tf_op jit(solution)/shard_map/all_to_all | solution.py:48
  161.8 10.4 %collective-permute-start.21 = (f32[128,256]{1,0:T(8,128)}, f32[128,256]{1,0:T(8,128)S(1)}, u32[]{:S(2)}, u32[]{:S(2)}) collective-permute-start(f32[128,256]{1,0:T(8,128)} %get-tuple-element.64), channel_id=1, source_target_pairs={{0,12},{1,13},{2,14},{3,15},{4,0},{5,1},{6,2},{7,3},{8,4},{9,5},{1... | collective-permute-start | bytes 393224 | tf_op jit(solution)/shard_map/ppermute | solution.py:57
  162.7 9.6 %collective-permute-start.22 = (f32[128,256]{1,0:T(8,128)}, f32[128,256]{1,0:T(8,128)S(1)}, u32[]{:S(2)}, u32[]{:S(2)}) collective-permute-start(f32[128,256]{1,0:T(8,128)} %get-tuple-element.65), channel_id=1, source_target_pairs={{0,8},{1,9},{2,10},{3,11},{4,12},{5,13},{6,14},{7,15},{8,0},{9,1},... | collective-permute-start | bytes 393224 | tf_op jit(solution)/shard_map/ppermute | solution.py:57
  168.7 11.8 %all-to-all-start.8 = ((f32[16,16,128]{2,1,0:T(8,128)}), f32[16,16,128]{2,1,0:T(8,128)S(1)}, u32[]{:S(2)}, u32[]{:S(2)}) async-start(f32[16,16,128]{2,1,0:T(8,128)} %shard_map.103), calls=%async_computation.8 | async-start | bytes 262144 | tf_op jit(solution)/shard_map/all_to_all | solution.py:48
  (5 other events, 43.4 us)
where the time goes:
time: 190 us; the launch traced here: 189 us
  starting transfers between devices  92.1 us (48%)
  Pallas kernels  75.7 us (40%)
  waiting for transfers between devices  14.9 us (8%)
  local copies, waits for them, and re-layouts  4.13 us (2%)
    pallas_call x19, Pallas kernels, call(): pl.pallas_call(kernel, out_shape=outs, cost_estimate=pl.CostEstimate(flop...  75.7 us
    all_to_all x9, starting transfers between devices, exchange(): return lax.all_to_all(copies, axis, split_axis=0, concat_axis=0, tiled=True)  61.7 us
    ppermute x24, starting transfers between devices, shifted(): return lax.ppermute(value, 'sib', pairs)  30.4 us
    all_to_all x9, waiting for transfers between devices, exchange(): return lax.all_to_all(copies, axis, split_axis=0, concat_axis=0, tiled=True)  13 us
    gather x1, local copies, waits for them, and re-layouts, shards(): targets.at[ordering].get(unique_indices=True, mode='promise_in_bounds')  4.1 us
  transfers between devices with their start and end apart: 33, of which 8 were waited for; matrix products, arithmetic and copies ran while one was open for 3% of the time, Pallas kernels for 29%

commit v1 on v0

--- a/solution.py
+++ b/solution.py
@@ -12,6 +12,8 @@
 ITERS = 3
 SIDE = 4
 TILE = 256
+WIDE = 640
+AHEAD = 2
 VMEM_GRANT = 34 << 20
 
 step_size = 0.5
@@ -116,16 +118,12 @@
     return call(place_kernel, [((2, SIDE * SIDE, rank, width), bf16)], 0, *parts, near_by=SIDE - 1)[0]
 
 
-def bands(rows):
-    return rows // TILE
-
-
-def band(index):
-    return pl.ds(pl.multiple_of(index * TILE, TILE), TILE)
-
-
-def over_bands(rows, body):
-    lax.fori_loop(0, bands(rows), lambda k, _: body(k), None)
+def band(index, tile):
+    return pl.ds(pl.multiple_of(index * tile, tile), tile)
+
+
+def over_bands(count, body):
+    lax.fori_loop(0, count, lambda k, _: body(k), None)
 
 
 def copies_of(*ends):
@@ -144,8 +142,26 @@
 
 
 def banded(pairs, sems, index):
-    cut = band(index)
+    tile = pairs[0][0].shape[0] // sems.shape[1]
+    cut = band(index, tile)
     return copies_of(*((a.at[cut], b.at[cut], sems.at[n, index]) for n, (a, b) in enumerate(pairs)))
+
+
+def lead(pairs, sems):
+    for k in range(min(AHEAD, sems.shape[1])):
+        start(banded(pairs, sems, k))
+
+
+def stream(pairs, sems, body, ahead=AHEAD):
+    def step(k):
+        @pl.when(k + ahead < sems.shape[1])
+        def _():
+            start(banded(pairs, sems, k + ahead))
+
+        finish(banded(pairs, sems, k))
+        body(k)
+
+    over_bands(sems.shape[1], step)
 
 
 def add_up(total_ref, basis, weights):
@@ -174,13 +190,12 @@
     rows = basis.shape[0]
     pairs = ((targets_ref, targets), (basis_ref, basis))
     outgoing = ((split.at[0], split_ref.at[0]), (split.at[1], split_ref.at[1]))
-    over_bands(rows, lambda k: (start(banded(pairs, in_sems, k)), None)[1])
+    lead(pairs, in_sems)
     transfer = halves(transfer_ref[...])
     total[...] = jnp.zeros_like(total)
 
     def step(k):
-        cut = band(k)
-        finish(banded(pairs, in_sems, k))
+        cut = band(k, WIDE)
         both = jnp.concatenate([basis[cut, :], product(halves(basis[cut, :]), transfer)], axis=1)
         high, low = halves(both)
         split[0, cut, :] = high
@@ -188,9 +203,9 @@
         start(banded(outgoing, out_sems, k))
         add_up(total, (high, low), halves(step_size * targets[cut, :]))
 
-    over_bands(rows, step)
+    stream(pairs, in_sems, step)
     sent = send_up(total, leaf, group, leaf_ref, group_ref, end_sems)
-    over_bands(rows, lambda k: finish(banded(outgoing, out_sems, k)))
+    over_bands(rows // WIDE, lambda k: finish(banded(outgoing, out_sems, k)))
     finish(sent)
 
 
@@ -214,8 +229,8 @@
             pltpu.VMEM(*outs[0]),
             pltpu.VMEM((2 * rank, columns), f32),
             *(pltpu.VMEM(*out) for out in outs[1:]),
-            DMA((2, bands(rows))),
-            DMA((2, bands(rows))),
+            DMA((2, rows // WIDE)),
+            DMA((2, rows // WIDE)),
             DMA((2,)),
         ],
     )
@@ -235,12 +250,11 @@
     rank = root_ref.shape[1]
     pairs = ((sum_ref, sums), (base_ref, base))
     pairs += ((along_ref.at[0], along.at[0]), (along_ref.at[1], along.at[1]))
-    over_bands(rows, lambda k: (start(banded(pairs, in_sems, k)), None)[1])
+    lead(pairs, in_sems)
     root = halves(root_ref[...].T)
 
     def step(k):
-        cut = band(k)
-        finish(banded(pairs, in_sems, k))
+        cut = band(k, WIDE)
         high, low = along[0, cut, :], along[1, cut, :]
         fitted = jnp.tanh(sums[cut, :] + product((along[0, cut, rank:], along[1, cut, rank:]), root))
         weights = base[cut, :] - step_size * fitted
@@ -252,24 +266,24 @@
             start(banded(outgoing, out_sems, k))
             add_up(total, (high, low), halves(weights))
 
-    over_bands(rows, step)
+    stream(pairs, in_sems, step)
     if last:
         order = order_ref[...]
 
         def scatter(k):
-            cut = band(k)
-            positions = lax.broadcasted_iota(jnp.int32, (TILE, rows), 0) + k * TILE
+            cut = band(k, WIDE)
+            positions = lax.broadcasted_iota(jnp.int32, (WIDE, rows), 0) + k * WIDE
             chosen = jnp.where(positions == order, 1.0, 0.0).astype(bf16)
             parts = jnp.dot(chosen, split[...], preferred_element_type=f32)
             sums[cut, :] = parts[:, :columns] + parts[:, columns : 2 * columns]
             base[cut, :] = parts[:, 2 * columns : 3 * columns] + parts[:, 3 * columns :]
             start(banded(outgoing, out_sems, k))
 
-        over_bands(rows, scatter)
+        over_bands(rows // WIDE, scatter)
     else:
         sent = send_up(total, leaf, group, leaf_ref, group_ref, end_sems)
         finish(sent)
-    over_bands(rows, lambda k: finish(banded(outgoing, out_sems, k)))
+    over_bands(rows // WIDE, lambda k: finish(banded(outgoing, out_sems, k)))
 
 
 def fit(last, sums, base, along, root, order):
@@ -277,7 +291,7 @@
     rank = root.shape[1]
     state = ((rows, columns), f32)
     scratch = [pltpu.VMEM(*state)] * 2 + [pltpu.VMEM(along.shape, bf16)]
-    sems = [DMA((4, bands(rows))), DMA((2, bands(rows)))]
+    sems = [DMA((4, rows // WIDE)), DMA((2, rows // WIDE))]
     if last:
         outs = [state, state]
         scratch += [pltpu.VMEM((rows, 4 * columns), bf16)]
@@ -326,17 +340,20 @@
         pairs = ((given[1].at[0], split.at[0]), (given[1].at[1], split.at[1]), (old_ref, old))
     arrived += copies_of((along_ref.at[:, :, pl.ds(0, rank)], leaf, start_sems.at[1]))
     start(arrived)
-    over_bands(rows, lambda k: (start(banded(pairs, in_sems, k)), None)[1])
+    start(banded(pairs, in_sems, 0))
     total = siblings[0][...]
     for ref in siblings[1:]:
         total = total + ref[...]
     total = halves(total)
-    finish(arrived)
+    finish(arrived[:1])
+    ahead = AHEAD + 1 if first else AHEAD
+    for k in range(1, ahead):
+        start(banded(pairs, in_sems, k))
     ready[0], ready[1] = halves(step_size * old[...] if first else now[...])
+    finish(arrived[1:])
 
     def step(k):
-        cut = band(k)
-        finish(banded(pairs, in_sems, k))
+        cut = band(k, TILE)
         if first:
             split[0, cut, :], split[1, cut, :] = halves(block[cut, :])
         weights = step_size * old[cut, :] if first else now[cut, :]
@@ -345,8 +362,8 @@
         base[cut, :] = weights - step_size * shrink_rate * weights + step_size * old[cut, :]
         start(banded(outgoing, out_sems, k))
 
-    over_bands(rows, step)
-    over_bands(rows, lambda k: finish(banded(outgoing, out_sems, k)))
+    stream(pairs, in_sems, step, ahead)
+    over_bands(rows // TILE, lambda k: finish(banded(outgoing, out_sems, k)))
 
 
 def near_sum(blocks, weights, targets, along, siblings):
@@ -371,42 +388,47 @@
         near_by=SIDE - 1,
         out_specs=[HBM] * (3 if first else 2),
         scratch_shapes=[pltpu.VMEM(*shape) for shape in shapes]
-        + [DMA((3, bands(rows))), DMA((4, bands(rows))), DMA((2,))],
+        + [DMA((3, rows // TILE)), DMA((4, rows // TILE)), DMA((2,))],
     )
 
 
 def sibling_kernel(split_ref, *refs):
     parts, (first_ref, *out_refs) = refs[:SIDE], refs[SIDE : 2 * SIDE]
-    split, sums, in_sem, out_sems = refs[2 * SIDE :]
+    split, given, sums, in_sems, out_sems = refs[2 * SIDE :]
     rank = parts[0].shape[0]
-    arriving = start(copies_of((split_ref, split, in_sem)))
-    coefficients = halves(jnp.concatenate([ref[...] for ref in parts]))
-    finish(arriving)
+    rows = [pl.ds(k * rank, rank) for k in range(SIDE)]
+    arriving = start(
+        copies_of(
+            *((part, given.at[cut], in_sems.at[k]) for k, (part, cut) in enumerate(zip(parts, rows))),
+            (split_ref, split, in_sems.at[SIDE]),
+        )
+    )
+    finish(arriving[:SIDE])
+    coefficients = halves(given[...])
+    finish(arriving[SIDE:])
     sums[...] = product((split[0], split[1]), coefficients)
-    outs = enumerate(out_refs, 1)
-    sent = start(
-        copies_of(*((sums.at[pl.ds(k * rank, rank)], out, out_sems.at[k - 1]) for k, out in outs))
-    )
-    first_ref[...] = sums[:rank, :]
-    finish(sent)
+    outs = enumerate((first_ref, *out_refs))
+    finish(start(copies_of(*((sums.at[rows[k]], out, out_sems.at[k]) for k, out in outs))))
 
 
 def sibling_sums(couplings, parts):
     rank, columns = parts[0].shape
+    whole = pltpu.VMEM((SIDE * rank, columns), f32)
     return call(
         sibling_kernel,
         [((rank, columns), f32)] * SIDE,
         6 * SIDE * SIDE * rank * rank * columns,
         couplings,
         *parts,
-        in_specs=[HBM] + [VMEM] * SIDE,
+        in_specs=[HBM] + [pl.BlockSpec(memory_space=pl.ANY)] * SIDE,
         near_by=SIDE - 1,
-        out_specs=[VMEM] + [HBM] * (SIDE - 1),
+        out_specs=[HBM] * SIDE,
         scratch_shapes=[
             pltpu.VMEM(couplings.shape, bf16),
-            pltpu.VMEM((SIDE * rank, columns), f32),
-            DMA(()),
-            DMA((SIDE - 1,)),
+            whole,
+            whole,
+            DMA((SIDE + 1,)),
+            DMA((SIDE,)),
         ],
     )
 

time: 190 us -> 187 us (0.984)
  Pallas kernels: 75.7 us -> 71.1 us
  waiting for transfers between devices: 14.9 us -> 17.7 us
    pallas_call x19, Pallas kernels: 75.7 us -> 71.1 us  [call(): pl.pallas_call(kernel, out_shape=outs, cost_estimate=pl.CostEstimate(flop...]
    all_to_all x9, waiting for transfers between devices: 13 us -> 15.8 us  [exchange(): return lax.all_to_all(copies, axis, split_axis=0, concat_axis=0, tiled=True)]
  transfers between devices with their start and end apart: 33 -> 33, of which waited for: 8 -> 7; matrix products, arithmetic and copies ran while one was open for 3% -> 3% of each run, Pallas kernels for 29% -> 28%
where the time goes in v1:
time: 187 us; the launch traced here: 185 us
  starting transfers between devices  90.4 us (48%)
  Pallas kernels  71.1 us (38%)
  waiting for transfers between devices  17.7 us (9%)
  local copies, waits for them, and re-layouts  4.13 us (2%)
    pallas_call x19, Pallas kernels, call(): pl.pallas_call(kernel, out_shape=outs, cost_estimate=pl.CostEstimate(flop...  71.1 us
    all_to_all x9, starting transfers between devices, exchange(): return lax.all_to_all(copies, axis, split_axis=0, concat_axis=0, tiled=True)  60.2 us
    ppermute x24, starting transfers between devices, shifted(): return lax.ppermute(value, 'sib', pairs)  30.2 us
    all_to_all x9, waiting for transfers between devices, exchange(): return lax.all_to_all(copies, axis, split_axis=0, concat_axis=0, tiled=True)  15.8 us
    gather x1, local copies, waits for them, and re-layouts, shards(): targets.at[ordering].get(unique_indices=True, mode='promise_in_bounds')  4.1 us
  transfers between devices with their start and end apart: 33, of which 7 were waited for; matrix products, arithmetic and copies ran while one was open for 3% of the time, Pallas kernels for 28%

profile of v1, /device:TPU:1, one launch (start us, length us, event | category | flops | bytes accessed | tf_op | source)
XLA Modules:
  0.0 185.2 jit_solution(1741333730445670090)
XLA Ops:
  0.6 2.5 %shard_map.87 = (f32[128,512]{1,0:T(8,128)}, f32[128,640]{1,0:T(8,128)}, f32[128,640]{1,0:T(8,128)}, f32[128,640]{1,0:T(8,128)}) custom-call(f32[128,2048]{1,0:T(8,128)} %row_ref.1, f32[128,128]{1,0:T(8,128)} %top_ref.3), custom_call_target="tpu_custom_call" | custom-call | bytes 2359296 | tf_op jit(solution)/shard_map/pallas_call | solution.py:40
  5.3 2.6 %collective-permute-start.1 = (f32[128,640]{1,0:T(8,128)}, f32[128,640]{1,0:T(8,128)S(1)}, u32[]{:S(2)}, u32[]{:S(2)}) collective-permute-start(f32[128,640]{1,0:T(8,128)} %get-tuple-element.39), channel_id=1, source_target_pairs={{0,8},{1,9},{2,10},{3,11},{4,12},{5,13},{6,14},{7,15},{8,0},{9,1},... | collective-permute-start | bytes 983048 | tf_op jit(solution)/shard_map/ppermute | solution.py:59
  9.7 4.1 %gather_fusion = f32[1280,256]{1,0:T(8,128)} fusion(f32[1280,256]{1,0:T(8,128)S(1)} %copy-done, s32[2048]{0:T(1024)S(1)} %pad_clamp_fusion), kind=kCustom, calls=%fused_computation | custom fusion | bytes 2626560 | tf_op jit(solution)/shard_map/gather | solution.py:471
  13.8 3.9 %shard_map.86 = (bf16[2,1280,256]{2,1,0:T(8,128)(2,1)}, f32[128,256]{1,0:T(8,128)}, f32[256,128]{1,0:T(8,128)}) custom-call(f32[1280,256]{1,0:T(8,128)} %gather_fusion, f32[1280,128]{1,0:T(8,128)} %basis_ref.1, f32[128,128]{1,0:T(8,128)S(1)} %copy-done.2), custom_call_target="tpu_custom_call" | custom-call | flops 754974720 | bytes 3604480 | tf_op jit(solution)/shard_map/pallas_call | solution.py:40
  17.8 2.6 %collective-permute-start.5 = (f32[128,256]{1,0:T(8,128)}, f32[128,256]{1,0:T(8,128)S(1)}, u32[]{:S(2)}, u32[]{:S(2)}) collective-permute-start(f32[128,256]{1,0:T(8,128)} %get-tuple-element.42.refs_0_), channel_id=1, source_target_pairs={{0,3},{1,0},{2,1},{3,2},{4,7},{5,4},{6,5},{7,6},{8,11},{9,8},{10,9... | collective-permute-start | bytes 393224 | tf_op jit(solution)/shard_map/ppermute | solution.py:59
  24.4 2.5 %collective-permute-start.11 = (f32[4,128,128]{2,1,0:T(8,128)}, f32[4,128,128]{2,1,0:T(8,128)S(1)}, u32[]{:S(2)}, u32[]{:S(2)}) collective-permute-start(f32[4,128,128]{2,1,0:T(8,128)} %get-tuple-element.49.refs_0_), channel_id=1, source_target_pairs={{0,3},{1,0},{2,1},{3,2},{4,7},{5,4},{6,5},{7,6},{8,11},{9,8},{10,9... | collective-permute-start | bytes 786440 | tf_op jit(solution)/shard_map/ppermute | solution.py:59
  26.9 4.5 %all-to-all-start = ((f32[16,16,128]{2,1,0:T(8,128)}), f32[16,16,128]{2,1,0:T(8,128)S(1)}, u32[]{:S(2)}, u32[]{:S(2)}) async-start(f32[16,16,128]{2,1,0:T(8,128)} %bitcast.1), calls=%async_computation | async-start | bytes 262144 | tf_op jit(solution)/shard_map/all_to_all | solution.py:50
  31.4 3.0 %collective-permute-start.4 = (f32[128,256]{1,0:T(8,128)S(1)}, f32[128,256]{1,0:T(8,128)S(1)}, u32[]{:S(2)}, u32[]{:S(2)}) collective-permute-start(f32[128,256]{1,0:T(8,128)S(1)} %copy-done.3), channel_id=1, source_target_pairs={{0,2},{1,3},{2,0},{3,1},{4,6},{5,7},{6,4},{7,5},{8,10},{9,11},{10,... | collective-permute-start | bytes 393224 | tf_op jit(solution)/shard_map/ppermute | solution.py:59
  38.9 11.9 %all-to-all-start.1 = ((f32[16,16,128]{2,1,0:T(8,128)}), f32[16,16,128]{2,1,0:T(8,128)S(1)}, u32[]{:S(2)}, u32[]{:S(2)}) async-start(f32[16,16,128]{2,1,0:T(8,128)} %shard_map.92), calls=%async_computation.1 | async-start | bytes 262144 | tf_op jit(solution)/shard_map/all_to_all | solution.py:50
  50.8 3.3 %shard_map.89 = (f32[128,256]{1,0:T(8,128)}, f32[128,256]{1,0:T(8,128)}, f32[128,256]{1,0:T(8,128)}, f32[128,256]{1,0:T(8,128)}) custom-call(bf16[2,512,512]{2,1,0:T(8,128)(2,1)} %get-tuple-element.41.split_ref, f32[128,256]{1,0:T(8,128)} %get-tuple-element.42.refs_0_, f32[128,256]{1,0:T(8,128)S(1)} %collective-permute-done.3.refs_1_, ...), custom_call_target="tpu_custom_call" | custom-call | flops 402653184 | bytes 2097152 | tf_op jit(solution)/shard_map/pallas_call | solution.py:40
  56.6 2.3 %shard_map.91.split_ref = bf16[2,16,128,128]{3,2,1,0:T(8,128)(2,1)} custom-call(f32[4,128,128]{2,1,0:T(8,128)} %get-tuple-element.49.refs_0_, f32[4,128,128]{2,1,0:T(8,128)S(1)} %collective-permute-done.9.refs_1_, f32[4,128,128]{2,1,0:T(8,128)S(1)} %collective-permute-done.10.refs_2_, f32[4,128,128]{2,1,0:T(8,128)S(1)} %collective-permute-done.11.refs_3_), custom_call_target="tpu_custom_call" | custom-call | bytes 2097152 | tf_op jit(solution)/shard_map/pallas_call | solution.py:40
  61.9 4.4 %all-to-all-start.2 = ((f32[16,16,128]{2,1,0:T(8,128)}), f32[16,16,128]{2,1,0:T(8,128)S(1)}, u32[]{:S(2)}, u32[]{:S(2)}) async-start(f32[16,16,128]{2,1,0:T(8,128)} %shard_map.93), calls=%async_computation.2 | async-start | bytes 262144 | tf_op jit(solution)/shard_map/all_to_all | solution.py:50
  66.3 8.4 %shard_map.90 = (f32[1280,256]{1,0:T(8,128)}, f32[1280,256]{1,0:T(8,128)}, bf16[2,1280,1280]{2,1,0:T(8,128)(2,1)}) custom-call(f32[1280,256]{1,0:T(8,128)} %gather_fusion, f32[1280,1280]{1,0:T(8,128)} %refs_1_.1, bf16[2,1280,256]{2,1,0:T(8,128)(2,1)} %get-tuple-element.36.refs_2_.refs_3_, f32[128,256]{1,0:T(8,128)} %get-tuple-element.43.refs_3_, ...), custom_call_target="tpu_custom_call" | custom-call | flops 2516582400 | bytes 18874368 | tf_op jit(solution)/shard_map/pallas_call | solution.py:40
  74.8 4.8 %shard_map.94 = (f32[1280,256]{1,0:T(8,128)}, f32[128,256]{1,0:T(8,128)}, f32[256,128]{1,0:T(8,128)}) custom-call(f32[1280,256]{1,0:T(8,128)} %get-tuple-element.47.refs_0_, f32[1280,256]{1,0:T(8,128)} %get-tuple-element.48.refs_1_, bf16[2,1280,256]{2,1,0:T(8,128)(2,1)} %get-tuple-element.36.refs_2_.refs_3_, f32[256,128]{1,0:T(8,128)S(1)} %bitcast.9), custom_call_target="tpu_custom_call" | custom-call | flops 754974720 | bytes 5636096 | tf_op jit(solution)/shard_map/pallas_call | solution.py:40
  79.5 6.7 %all-to-all-start.3 = ((f32[16,16,128]{2,1,0:T(8,128)}), f32[16,16,128]{2,1,0:T(8,128)S(1)}, u32[]{:S(2)}, u32[]{:S(2)}) async-start(f32[16,16,128]{2,1,0:T(8,128)} %bitcast.11), calls=%async_computation.3 | async-start | bytes 262144 | tf_op jit(solution)/shard_map/all_to_all | solution.py:50
  86.2 2.6 %collective-permute-start.14 = (f32[128,256]{1,0:T(8,128)}, f32[128,256]{1,0:T(8,128)S(1)}, u32[]{:S(2)}, u32[]{:S(2)}) collective-permute-start(f32[128,256]{1,0:T(8,128)} %get-tuple-element.53.refs_0_), channel_id=1, source_target_pairs={{0,3},{1,0},{2,1},{3,2},{4,7},{5,4},{6,5},{7,6},{8,11},{9,8},{10,9... | collective-permute-start | bytes 393224 | tf_op jit(solution)/shard_map/ppermute | solution.py:59
  89.9 3.1 %all-to-all-done.3.parts_ref = f32[16,16,128]{2,1,0:T(8,128)S(1)} async-done(((f32[16,16,128]{2,1,0:T(8,128)}), f32[16,16,128]{2,1,0:T(8,128)S(1)}, u32[]{:S(2)}, u32[]{:S(2)}) %all-to-all-start.3) | async-done | bytes 131104 | tf_op jit(solution)/shard_map/all_to_all | solution.py:50
  93.7 10.6 %all-to-all-start.4 = ((f32[16,16,128]{2,1,0:T(8,128)}), f32[16,16,128]{2,1,0:T(8,128)S(1)}, u32[]{:S(2)}, u32[]{:S(2)}) async-start(f32[16,16,128]{2,1,0:T(8,128)} %shard_map.97), calls=%async_computation.4 | async-start | bytes 262144 | tf_op jit(solution)/shard_map/all_to_all | solution.py:50
  104.4 3.2 %shard_map.95 = (f32[128,256]{1,0:T(8,128)}, f32[128,256]{1,0:T(8,128)}, f32[128,256]{1,0:T(8,128)}, f32[128,256]{1,0:T(8,128)}) custom-call(bf16[2,512,512]{2,1,0:T(8,128)(2,1)} %get-tuple-element.41.split_ref, f32[128,256]{1,0:T(8,128)} %get-tuple-element.53.refs_0_, f32[128,256]{1,0:T(8,128)S(1)} %collective-permute-done.12.refs_1_, ...), custom_call_target="tpu_custom_call" | custom-call | flops 402653184 | bytes 2097152 | tf_op jit(solution)/shard_map/pallas_call | solution.py:40
  109.1 4.1 %all-to-all-done.4.parts_ref = f32[16,16,128]{2,1,0:T(8,128)S(1)} async-done(((f32[16,16,128]{2,1,0:T(8,128)}), f32[16,16,128]{2,1,0:T(8,128)S(1)}, u32[]{:S(2)}, u32[]{:S(2)}) %all-to-all-start.4) | async-done | bytes 131104 | tf_op jit(solution)/shard_map/all_to_all | solution.py:50
  115.4 3.5 %all-to-all-start.5 = ((f32[16,16,128]{2,1,0:T(8,128)}), f32[16,16,128]{2,1,0:T(8,128)S(1)}, u32[]{:S(2)}, u32[]{:S(2)}) async-start(f32[16,16,128]{2,1,0:T(8,128)} %shard_map.98), calls=%async_computation.5 | async-start | bytes 262144 | tf_op jit(solution)/shard_map/all_to_all | solution.py:50
  119.0 8.2 %shard_map.96 = (f32[1280,256]{1,0:T(8,128)}, f32[1280,256]{1,0:T(8,128)}) custom-call(f32[1280,256]{1,0:T(8,128)} %gather_fusion, f32[1280,256]{1,0:T(8,128)} %get-tuple-element.51.refs_1_, bf16[2,1280,1280]{2,1,0:T(8,128)(2,1)} %get-tuple-element.52.refs_2_, bf16[2,1280,256]{2,1,0:T(8,128)(2,1)} %get-tuple-element.36.refs_2_.refs_3_, ...), custom_call_target="tpu_custom_call" | custom-call | flops 2516582400 | bytes 13631488 | tf_op jit(solution)/shard_map/pallas_call | solution.py:40
  127.2 4.8 %shard_map.99 = (f32[1280,256]{1,0:T(8,128)}, f32[128,256]{1,0:T(8,128)}, f32[256,128]{1,0:T(8,128)}) custom-call(f32[1280,256]{1,0:T(8,128)} %get-tuple-element.58.refs_0_, f32[1280,256]{1,0:T(8,128)} %get-tuple-element.59.refs_1_, bf16[2,1280,256]{2,1,0:T(8,128)(2,1)} %get-tuple-element.36.refs_2_.refs_3_, f32[256,128]{1,0:T(8,128)S(1)} %bitcast.8), custom_call_target="tpu_custom_call" | custom-call | flops 754974720 | bytes 5636096 | tf_op jit(solution)/shard_map/pallas_call | solution.py:40
  132.0 6.6 %all-to-all-start.6 = ((f32[16,16,128]{2,1,0:T(8,128)}), f32[16,16,128]{2,1,0:T(8,128)S(1)}, u32[]{:S(2)}, u32[]{:S(2)}) async-start(f32[16,16,128]{2,1,0:T(8,128)} %bitcast.12), calls=%async_computation.6 | async-start | bytes 262144 | tf_op jit(solution)/shard_map/all_to_all | solution.py:50
  138.6 2.6 %collective-permute-start.20 = (f32[128,256]{1,0:T(8,128)}, f32[128,256]{1,0:T(8,128)S(1)}, u32[]{:S(2)}, u32[]{:S(2)}) collective-permute-start(f32[128,256]{1,0:T(8,128)} %get-tuple-element.62.refs_0_), channel_id=1, source_target_pairs={{0,3},{1,0},{2,1},{3,2},{4,7},{5,4},{6,5},{7,6},{8,11},{9,8},{10,9... | collective-permute-start | bytes 393224 | tf_op jit(solution)/shard_map/ppermute | solution.py:59
  142.3 3.1 %all-to-all-done.6.parts_ref = f32[16,16,128]{2,1,0:T(8,128)S(1)} async-done(((f32[16,16,128]{2,1,0:T(8,128)}), f32[16,16,128]{2,1,0:T(8,128)S(1)}, u32[]{:S(2)}, u32[]{:S(2)}) %all-to-all-start.6) | async-done | bytes 131104 | tf_op jit(solution)/shard_map/all_to_all | solution.py:50
  146.1 8.5 %all-to-all-start.7 = ((f32[16,16,128]{2,1,0:T(8,128)}), f32[16,16,128]{2,1,0:T(8,128)S(1)}, u32[]{:S(2)}, u32[]{:S(2)}) async-start(f32[16,16,128]{2,1,0:T(8,128)} %shard_map.102), calls=%async_computation.7 | async-start | bytes 262144 | tf_op jit(solution)/shard_map/all_to_all | solution.py:50
  154.7 3.2 %shard_map.100 = (f32[128,256]{1,0:T(8,128)}, f32[128,256]{1,0:T(8,128)}, f32[128,256]{1,0:T(8,128)}, f32[128,256]{1,0:T(8,128)}) custom-call(bf16[2,512,512]{2,1,0:T(8,128)(2,1)} %get-tuple-element.41.split_ref, f32[128,256]{1,0:T(8,128)} %get-tuple-element.62.refs_0_, f32[128,256]{1,0:T(8,128)S(1)} %collective-permute-done.18.refs_1_, ...), custom_call_target="tpu_custom_call" | custom-call | flops 402653184 | bytes 2097152 | tf_op jit(solution)/shard_map/pallas_call | solution.py:40
  159.4 4.1 %all-to-all-done.7.parts_ref = f32[16,16,128]{2,1,0:T(8,128)S(1)} async-done(((f32[16,16,128]{2,1,0:T(8,128)}), f32[16,16,128]{2,1,0:T(8,128)S(1)}, u32[]{:S(2)}, u32[]{:S(2)}) %all-to-all-start.7) | async-done | bytes 131104 | tf_op jit(solution)/shard_map/all_to_all | solution.py:50
  165.8 3.5 %all-to-all-start.8 = ((f32[16,16,128]{2,1,0:T(8,128)}), f32[16,16,128]{2,1,0:T(8,128)S(1)}, u32[]{:S(2)}, u32[]{:S(2)}) async-start(f32[16,16,128]{2,1,0:T(8,128)} %shard_map.103), calls=%async_computation.8 | async-start | bytes 262144 | tf_op jit(solution)/shard_map/all_to_all | solution.py:50
  169.3 8.2 %shard_map.101 = (f32[1280,256]{1,0:T(8,128)}, f32[1280,256]{1,0:T(8,128)}) custom-call(f32[1280,256]{1,0:T(8,128)} %gather_fusion, f32[1280,256]{1,0:T(8,128)} %get-tuple-element.61.refs_1_, bf16[2,1280,1280]{2,1,0:T(8,128)(2,1)} %get-tuple-element.52.refs_2_, bf16[2,1280,256]{2,1,0:T(8,128)(2,1)} %get-tuple-element.36.refs_2_.refs_3_, ...), custom_call_target="tpu_custom_call" | custom-call | flops 2516582400 | bytes 13631488 | tf_op jit(solution)/shard_map/pallas_call | solution.py:40
  177.6 7.4 %shard_map.104 = (f32[1280,256]{1,0:T(8,128)}, f32[1280,256]{1,0:T(8,128)}) custom-call(f32[1280,256]{1,0:T(8,128)} %get-tuple-element.67.refs_0_, f32[1280,256]{1,0:T(8,128)} %get-tuple-element.68.refs_1_, bf16[2,1280,256]{2,1,0:T(8,128)(2,1)} %get-tuple-element.36.refs_2_.refs_3_, f32[256,128]{1,0:T(8,128)S(1)} %bitcast.10, s32[1,1280]{1,0:T(1,128)S(1)} %copy-done.1), custom_call_target="tpu_custom_call" | custom-call | flops 754974720 | bytes 6689792 | tf_op jit(solution)/shard_map/pallas_call | solution.py:40
  (64 shorter events, 29.2 us)
Async XLA Ops:
  3.2 17.2 %collective-permute-start = (f32[128,640]{1,0:T(8,128)}, f32[128,640]{1,0:T(8,128)S(1)}, u32[]{:S(2)}, u32[]{:S(2)}) collective-permute-start(f32[128,640]{1,0:T(8,128)} %get-tuple-element.38), channel_id=1, source_target_pairs={{0,4},{1,5},{2,6},{3,7},{4,8},{5,9},{6,10},{7,11},{8,12},{9,13},{1... | collective-permute-start | bytes 983048 | tf_op jit(solution)/shard_map/ppermute | solution.py:59
  5.3 17.0 %collective-permute-start.1 = (f32[128,640]{1,0:T(8,128)}, f32[128,640]{1,0:T(8,128)S(1)}, u32[]{:S(2)}, u32[]{:S(2)}) collective-permute-start(f32[128,640]{1,0:T(8,128)} %get-tuple-element.39), channel_id=1, source_target_pairs={{0,8},{1,9},{2,10},{3,11},{4,12},{5,13},{6,14},{7,15},{8,0},{9,1},... | collective-permute-start | bytes 983048 | tf_op jit(solution)/shard_map/ppermute | solution.py:59
  7.9 14.4 %collective-permute-start.2 = (f32[128,640]{1,0:T(8,128)}, f32[128,640]{1,0:T(8,128)S(1)}, u32[]{:S(2)}, u32[]{:S(2)}) collective-permute-start(f32[128,640]{1,0:T(8,128)} %get-tuple-element.40), channel_id=1, source_target_pairs={{0,12},{1,13},{2,14},{3,15},{4,0},{5,1},{6,2},{7,3},{8,4},{9,5},{1... | collective-permute-start | bytes 983048 | tf_op jit(solution)/shard_map/ppermute | solution.py:59
  17.8 18.6 %collective-permute-start.5 = (f32[128,256]{1,0:T(8,128)}, f32[128,256]{1,0:T(8,128)S(1)}, u32[]{:S(2)}, u32[]{:S(2)}) collective-permute-start(f32[128,256]{1,0:T(8,128)} %get-tuple-element.42.refs_0_), channel_id=1, source_target_pairs={{0,3},{1,0},{2,1},{3,2},{4,7},{5,4},{6,5},{7,6},{8,11},{9,8},{10,9... | collective-permute-start | bytes 393224 | tf_op jit(solution)/shard_map/ppermute | solution.py:59
  24.4 31.7 %collective-permute-start.11 = (f32[4,128,128]{2,1,0:T(8,128)}, f32[4,128,128]{2,1,0:T(8,128)S(1)}, u32[]{:S(2)}, u32[]{:S(2)}) collective-permute-start(f32[4,128,128]{2,1,0:T(8,128)} %get-tuple-element.49.refs_0_), channel_id=1, source_target_pairs={{0,3},{1,0},{2,1},{3,2},{4,7},{5,4},{6,5},{7,6},{8,11},{9,8},{10,9... | collective-permute-start | bytes 786440 | tf_op jit(solution)/shard_map/ppermute | solution.py:59
  26.9 11.3 %all-to-all-start = ((f32[16,16,128]{2,1,0:T(8,128)}), f32[16,16,128]{2,1,0:T(8,128)S(1)}, u32[]{:S(2)}, u32[]{:S(2)}) async-start(f32[16,16,128]{2,1,0:T(8,128)} %bitcast.1), calls=%async_computation | async-start | bytes 262144 | tf_op jit(solution)/shard_map/all_to_all | solution.py:50
  31.4 19.4 %collective-permute-start.4 = (f32[128,256]{1,0:T(8,128)S(1)}, f32[128,256]{1,0:T(8,128)S(1)}, u32[]{:S(2)}, u32[]{:S(2)}) collective-permute-start(f32[128,256]{1,0:T(8,128)S(1)} %copy-done.3), channel_id=1, source_target_pairs={{0,2},{1,3},{2,0},{3,1},{4,6},{5,7},{6,4},{7,5},{8,10},{9,11},{10,... | collective-permute-start | bytes 393224 | tf_op jit(solution)/shard_map/ppermute | solution.py:59
  34.3 16.5 %collective-permute-start.3 = (f32[128,256]{1,0:T(8,128)S(1)}, f32[128,256]{1,0:T(8,128)S(1)}, u32[]{:S(2)}, u32[]{:S(2)}) collective-permute-start(f32[128,256]{1,0:T(8,128)S(1)} %copy-done.3), channel_id=1, source_target_pairs={{0,1},{1,2},{2,3},{3,0},{4,5},{5,6},{6,7},{7,4},{8,9},{9,10},{10,1... | collective-permute-start | bytes 393224 | tf_op jit(solution)/shard_map/ppermute | solution.py:59
  34.6 22.0 %collective-permute-start.10 = (f32[4,128,128]{2,1,0:T(8,128)}, f32[4,128,128]{2,1,0:T(8,128)S(1)}, u32[]{:S(2)}, u32[]{:S(2)}) collective-permute-start(f32[4,128,128]{2,1,0:T(8,128)} %get-tuple-element.49.refs_0_), channel_id=1, source_target_pairs={{0,2},{1,3},{2,0},{3,1},{4,6},{5,7},{6,4},{7,5},{8,10},{9,11},{10,... | collective-permute-start | bytes 786440 | tf_op jit(solution)/shard_map/ppermute | solution.py:59
  36.4 20.2 %collective-permute-start.9 = (f32[4,128,128]{2,1,0:T(8,128)}, f32[4,128,128]{2,1,0:T(8,128)S(1)}, u32[]{:S(2)}, u32[]{:S(2)}) collective-permute-start(f32[4,128,128]{2,1,0:T(8,128)} %get-tuple-element.49.refs_0_), channel_id=1, source_target_pairs={{0,1},{1,2},{2,3},{3,0},{4,5},{5,6},{6,7},{7,4},{8,9},{9,10},{10,1... | collective-permute-start | bytes 786440 | tf_op jit(solution)/shard_map/ppermute | solution.py:59
  38.9 20.8 %all-to-all-start.1 = ((f32[16,16,128]{2,1,0:T(8,128)}), f32[16,16,128]{2,1,0:T(8,128)S(1)}, u32[]{:S(2)}, u32[]{:S(2)}) async-start(f32[16,16,128]{2,1,0:T(8,128)} %shard_map.92), calls=%async_computation.1 | async-start | bytes 262144 | tf_op jit(solution)/shard_map/all_to_all | solution.py:50
  54.1 12.3 %collective-permute-start.6 = (f32[128,256]{1,0:T(8,128)}, f32[128,256]{1,0:T(8,128)S(1)}, u32[]{:S(2)}, u32[]{:S(2)}) collective-permute-start(f32[128,256]{1,0:T(8,128)} %get-tuple-element.44), channel_id=1, source_target_pairs={{0,12},{1,13},{2,14},{3,15},{4,0},{5,1},{6,2},{7,3},{8,4},{9,5},{1... | collective-permute-start | bytes 393224 | tf_op jit(solution)/shard_map/ppermute | solution.py:59
  55.5 10.9 %collective-permute-start.7 = (f32[128,256]{1,0:T(8,128)}, f32[128,256]{1,0:T(8,128)S(1)}, u32[]{:S(2)}, u32[]{:S(2)}) collective-permute-start(f32[128,256]{1,0:T(8,128)} %get-tuple-element.45), channel_id=1, source_target_pairs={{0,8},{1,9},{2,10},{3,11},{4,12},{5,13},{6,14},{7,15},{8,0},{9,1},... | collective-permute-start | bytes 393224 | tf_op jit(solution)/shard_map/ppermute | solution.py:59
  56.0 10.3 %collective-permute-start.8 = (f32[128,256]{1,0:T(8,128)}, f32[128,256]{1,0:T(8,128)S(1)}, u32[]{:S(2)}, u32[]{:S(2)}) collective-permute-start(f32[128,256]{1,0:T(8,128)} %get-tuple-element.46), channel_id=1, source_target_pairs={{0,4},{1,5},{2,6},{3,7},{4,8},{5,9},{6,10},{7,11},{8,12},{9,13},{1... | collective-permute-start | bytes 393224 | tf_op jit(solution)/shard_map/ppermute | solution.py:59
  61.9 12.9 %all-to-all-start.2 = ((f32[16,16,128]{2,1,0:T(8,128)}), f32[16,16,128]{2,1,0:T(8,128)S(1)}, u32[]{:S(2)}, u32[]{:S(2)}) async-start(f32[16,16,128]{2,1,0:T(8,128)} %shard_map.93), calls=%async_computation.2 | async-start | bytes 262144 | tf_op jit(solution)/shard_map/all_to_all | solution.py:50
  79.5 13.5 %all-to-all-start.3 = ((f32[16,16,128]{2,1,0:T(8,128)}), f32[16,16,128]{2,1,0:T(8,128)S(1)}, u32[]{:S(2)}, u32[]{:S(2)}) async-start(f32[16,16,128]{2,1,0:T(8,128)} %bitcast.11), calls=%async_computation.3 | async-start | bytes 262144 | tf_op jit(solution)/shard_map/all_to_all | solution.py:50
  86.2 18.1 %collective-permute-start.14 = (f32[128,256]{1,0:T(8,128)}, f32[128,256]{1,0:T(8,128)S(1)}, u32[]{:S(2)}, u32[]{:S(2)}) collective-permute-start(f32[128,256]{1,0:T(8,128)} %get-tuple-element.53.refs_0_), channel_id=1, source_target_pairs={{0,3},{1,0},{2,1},{3,2},{4,7},{5,4},{6,5},{7,6},{8,11},{9,8},{10,9... | collective-permute-start | bytes 393224 | tf_op jit(solution)/shard_map/ppermute | solution.py:59
  88.8 15.6 %collective-permute-start.13 = (f32[128,256]{1,0:T(8,128)}, f32[128,256]{1,0:T(8,128)S(1)}, u32[]{:S(2)}, u32[]{:S(2)}) collective-permute-start(f32[128,256]{1,0:T(8,128)} %get-tuple-element.53.refs_0_), channel_id=1, source_target_pairs={{0,2},{1,3},{2,0},{3,1},{4,6},{5,7},{6,4},{7,5},{8,10},{9,11},{10,... | collective-permute-start | bytes 393224 | tf_op jit(solution)/shard_map/ppermute | solution.py:59
  89.4 15.0 %collective-permute-start.12 = (f32[128,256]{1,0:T(8,128)}, f32[128,256]{1,0:T(8,128)S(1)}, u32[]{:S(2)}, u32[]{:S(2)}) collective-permute-start(f32[128,256]{1,0:T(8,128)} %get-tuple-element.53.refs_0_), channel_id=1, source_target_pairs={{0,1},{1,2},{2,3},{3,0},{4,5},{5,6},{6,7},{7,4},{8,9},{9,10},{10,1... | collective-permute-start | bytes 393224 | tf_op jit(solution)/shard_map/ppermute | solution.py:59
  93.7 19.5 %all-to-all-start.4 = ((f32[16,16,128]{2,1,0:T(8,128)}), f32[16,16,128]{2,1,0:T(8,128)S(1)}, u32[]{:S(2)}, u32[]{:S(2)}) async-start(f32[16,16,128]{2,1,0:T(8,128)} %shard_map.97), calls=%async_computation.4 | async-start | bytes 262144 | tf_op jit(solution)/shard_map/all_to_all | solution.py:50
  107.5 11.4 %collective-permute-start.15 = (f32[128,256]{1,0:T(8,128)}, f32[128,256]{1,0:T(8,128)S(1)}, u32[]{:S(2)}, u32[]{:S(2)}) collective-permute-start(f32[128,256]{1,0:T(8,128)} %get-tuple-element.55), channel_id=1, source_target_pairs={{0,12},{1,13},{2,14},{3,15},{4,0},{5,1},{6,2},{7,3},{8,4},{9,5},{1... | collective-permute-start | bytes 393224 | tf_op jit(solution)/shard_map/ppermute | solution.py:59
  108.2 10.8 %collective-permute-start.16 = (f32[128,256]{1,0:T(8,128)}, f32[128,256]{1,0:T(8,128)S(1)}, u32[]{:S(2)}, u32[]{:S(2)}) collective-permute-start(f32[128,256]{1,0:T(8,128)} %get-tuple-element.56), channel_id=1, source_target_pairs={{0,8},{1,9},{2,10},{3,11},{4,12},{5,13},{6,14},{7,15},{8,0},{9,1},... | collective-permute-start | bytes 393224 | tf_op jit(solution)/shard_map/ppermute | solution.py:59
  108.9 10.1 %collective-permute-start.17 = (f32[128,256]{1,0:T(8,128)}, f32[128,256]{1,0:T(8,128)S(1)}, u32[]{:S(2)}, u32[]{:S(2)}) collective-permute-start(f32[128,256]{1,0:T(8,128)} %get-tuple-element.57), channel_id=1, source_target_pairs={{0,4},{1,5},{2,6},{3,7},{4,8},{5,9},{6,10},{7,11},{8,12},{9,13},{1... | collective-permute-start | bytes 393224 | tf_op jit(solution)/shard_map/ppermute | solution.py:59
  115.4 11.8 %all-to-all-start.5 = ((f32[16,16,128]{2,1,0:T(8,128)}), f32[16,16,128]{2,1,0:T(8,128)S(1)}, u32[]{:S(2)}, u32[]{:S(2)}) async-start(f32[16,16,128]{2,1,0:T(8,128)} %shard_map.98), calls=%async_computation.5 | async-start | bytes 262144 | tf_op jit(solution)/shard_map/all_to_all | solution.py:50
  132.0 13.5 %all-to-all-start.6 = ((f32[16,16,128]{2,1,0:T(8,128)}), f32[16,16,128]{2,1,0:T(8,128)S(1)}, u32[]{:S(2)}, u32[]{:S(2)}) async-start(f32[16,16,128]{2,1,0:T(8,128)} %bitcast.12), calls=%async_computation.6 | async-start | bytes 262144 | tf_op jit(solution)/shard_map/all_to_all | solution.py:50
  138.6 16.1 %collective-permute-start.20 = (f32[128,256]{1,0:T(8,128)}, f32[128,256]{1,0:T(8,128)S(1)}, u32[]{:S(2)}, u32[]{:S(2)}) collective-permute-start(f32[128,256]{1,0:T(8,128)} %get-tuple-element.62.refs_0_), channel_id=1, source_target_pairs={{0,3},{1,0},{2,1},{3,2},{4,7},{5,4},{6,5},{7,6},{8,11},{9,8},{10,9... | collective-permute-start | bytes 393224 | tf_op jit(solution)/shard_map/ppermute | solution.py:59
  141.2 13.5 %collective-permute-start.19 = (f32[128,256]{1,0:T(8,128)}, f32[128,256]{1,0:T(8,128)S(1)}, u32[]{:S(2)}, u32[]{:S(2)}) collective-permute-start(f32[128,256]{1,0:T(8,128)} %get-tuple-element.62.refs_0_), channel_id=1, source_target_pairs={{0,2},{1,3},{2,0},{3,1},{4,6},{5,7},{6,4},{7,5},{8,10},{9,11},{10,... | collective-permute-start | bytes 393224 | tf_op jit(solution)/shard_map/ppermute | solution.py:59
  141.7 12.9 %collective-permute-start.18 = (f32[128,256]{1,0:T(8,128)}, f32[128,256]{1,0:T(8,128)S(1)}, u32[]{:S(2)}, u32[]{:S(2)}) collective-permute-start(f32[128,256]{1,0:T(8,128)} %get-tuple-element.62.refs_0_), channel_id=1, source_target_pairs={{0,1},{1,2},{2,3},{3,0},{4,5},{5,6},{6,7},{7,4},{8,9},{9,10},{10,1... | collective-permute-start | bytes 393224 | tf_op jit(solution)/shard_map/ppermute | solution.py:59
  146.1 17.4 %all-to-all-start.7 = ((f32[16,16,128]{2,1,0:T(8,128)}), f32[16,16,128]{2,1,0:T(8,128)S(1)}, u32[]{:S(2)}, u32[]{:S(2)}) async-start(f32[16,16,128]{2,1,0:T(8,128)} %shard_map.102), calls=%async_computation.7 | async-start | bytes 262144 | tf_op jit(solution)/shard_map/all_to_all | solution.py:50
  157.9 11.4 %collective-permute-start.21 = (f32[128,256]{1,0:T(8,128)}, f32[128,256]{1,0:T(8,128)S(1)}, u32[]{:S(2)}, u32[]{:S(2)}) collective-permute-start(f32[128,256]{1,0:T(8,128)} %get-tuple-element.64), channel_id=1, source_target_pairs={{0,12},{1,13},{2,14},{3,15},{4,0},{5,1},{6,2},{7,3},{8,4},{9,5},{1... | collective-permute-start | bytes 393224 | tf_op jit(solution)/shard_map/ppermute | solution.py:59
  158.5 10.8 %collective-permute-start.22 = (f32[128,256]{1,0:T(8,128)}, f32[128,256]{1,0:T(8,128)S(1)}, u32[]{:S(2)}, u32[]{:S(2)}) collective-permute-start(f32[128,256]{1,0:T(8,128)} %get-tuple-element.65), channel_id=1, source_target_pairs={{0,8},{1,9},{2,10},{3,11},{4,12},{5,13},{6,14},{7,15},{8,0},{9,1},... | collective-permute-start | bytes 393224 | tf_op jit(solution)/shard_map/ppermute | solution.py:59
  165.8 11.8 %all-to-all-start.8 = ((f32[16,16,128]{2,1,0:T(8,128)}), f32[16,16,128]{2,1,0:T(8,128)S(1)}, u32[]{:S(2)}, u32[]{:S(2)}) async-start(f32[16,16,128]{2,1,0:T(8,128)} %shard_map.103), calls=%async_computation.8 | async-start | bytes 262144 | tf_op jit(solution)/shard_map/all_to_all | solution.py:50
  (5 other events, 45.1 us)

commit v2 on v1

--- a/solution.py
+++ b/solution.py
@@ -236,7 +236,11 @@
     )
 
 
-def fit_kernel(last, *refs):
+def carried(weights, targets):
+    return weights - step_size * shrink_rate * weights + step_size * targets
+
+
+def fit_kernel(first, last, *refs):
     sum_ref, base_ref, along_ref, root_ref, *refs = refs
     if last:
         order_ref, coeffs_ref, fitted_ref, sums, base, along, split, in_sems, out_sems = refs
@@ -257,7 +261,10 @@
         cut = band(k, WIDE)
         high, low = along[0, cut, :], along[1, cut, :]
         fitted = jnp.tanh(sums[cut, :] + product((along[0, cut, rank:], along[1, cut, rank:]), root))
-        weights = base[cut, :] - step_size * fitted
+        given = base[cut, :]
+        if first:
+            given = carried(step_size * given, given)
+        weights = given - step_size * fitted
         if last:
             for n, part in enumerate((*halves(weights), *halves(fitted))):
                 split[cut, n * columns : (n + 1) * columns] = part
@@ -286,7 +293,7 @@
     over_bands(rows // WIDE, lambda k: finish(banded(outgoing, out_sems, k)))
 
 
-def fit(last, sums, base, along, root, order):
+def fit(first, last, sums, base, along, root, order):
     rows, columns = sums.shape
     rank = root.shape[1]
     state = ((rows, columns), f32)
@@ -301,7 +308,7 @@
         scratch += [pltpu.VMEM(*out) for out in outs[1:]]
         sems += [DMA((2,))]
     return call(
-        functools.partial(fit_kernel, last),
+        functools.partial(fit_kernel, first, last),
         outs,
         18 * rows * columns * rank,
         sums,
@@ -320,17 +327,18 @@
     old_ref, *refs = refs
     given, refs = refs[: 1 if first else 2], refs[1 if first else 2 :]
     along_ref, *refs = refs
-    siblings, refs = refs[:SIDE], refs[SIDE:]
-    sum_ref, base_ref, *refs = refs
+    siblings, (sum_ref, *refs) = refs[:SIDE], refs[SIDE:]
     if first:
         split_ref, block, *refs = refs
+    else:
+        base_ref, *refs = refs
     old, sums, base, leaf, split, ready, *refs = refs
     if not first:
         now, *refs = refs
     in_sems, out_sems, start_sems = refs
     rank = siblings[0].shape[0]
     rows = sums.shape[0]
-    outgoing = ((sums, sum_ref), (base, base_ref))
+    outgoing = ((sums, sum_ref),) if first else ((sums, sum_ref), (base, base_ref))
     if first:
         arrived = copies_of((old_ref, old, start_sems.at[0]))
         pairs = ((given[0], block),)
@@ -356,10 +364,10 @@
         cut = band(k, TILE)
         if first:
             split[0, cut, :], split[1, cut, :] = halves(block[cut, :])
-        weights = step_size * old[cut, :] if first else now[cut, :]
         near = product((split[0, cut, :], split[1, cut, :]), (ready[0], ready[1]))
         sums[cut, :] = near + product((leaf[0, cut, :], leaf[1, cut, :]), total)
-        base[cut, :] = weights - step_size * shrink_rate * weights + step_size * old[cut, :]
+        if not first:
+            base[cut, :] = carried(now[cut, :], old[cut, :])
         start(banded(outgoing, out_sems, k))
 
     stream(pairs, in_sems, step, ahead)
@@ -377,7 +385,7 @@
     shapes += [] if first else [state]
     return call(
         functools.partial(near_kernel, first),
-        [state] * 2 + ([split] if first else []),
+        [state, split] if first else [state] * 2,
         6 * rows * rows * columns,
         targets,
         *(() if first else (weights,)),
@@ -386,7 +394,7 @@
         *siblings,
         in_specs=[HBM] * (3 if first else 4) + [VMEM] * SIDE,
         near_by=SIDE - 1,
-        out_specs=[HBM] * (3 if first else 2),
+        out_specs=[HBM] * 2,
         scratch_shapes=[pltpu.VMEM(*shape) for shape in shapes]
         + [DMA((3, rows // TILE)), DMA((4, rows // TILE)), DMA((2,))],
     )
@@ -488,9 +496,10 @@
         sums = [sums[0]] + [shifted(sums[ahead], -ahead, 0) for ahead in range(1, SIDE)]
         roots = root_copies(others, tops)
         root_whole = exchange(roots, "sib").reshape(columns, rank)
-        near, base, *split = near_sum(blocks, weights, tree_targets, along, sums)
-        blocks = split[0] if split else blocks
-        outs = fit(last, near, base, along, root_whole, leaf_order)
+        first = iteration == 0
+        near, other = near_sum(blocks, weights, tree_targets, along, sums)
+        base, blocks = (tree_targets, other) if first else (other, blocks)
+        outs = fit(first, last, near, base, along, root_whole, leaf_order)
         if not last:
             weights, leaf_part, group_part = outs
     return tuple(outs)

time: 187 us -> 186 us (level)
  no operation moved by 1% of the time
where the time goes in v2:
time: 186 us; the launch traced here: 185 us
  starting transfers between devices  90.4 us (49%)
  Pallas kernels  71 us (38%)
  waiting for transfers between devices  17.7 us (10%)
  local copies, waits for them, and re-layouts  4.13 us (2%)
    pallas_call x19, Pallas kernels, call(): pl.pallas_call(kernel, out_shape=outs, cost_estimate=pl.CostEstimate(flop...  71 us
    all_to_all x9, starting transfers between devices, exchange(): return lax.all_to_all(copies, axis, split_axis=0, concat_axis=0, tiled=True)  60.2 us
    ppermute x24, starting transfers between devices, shifted(): return lax.ppermute(value, 'sib', pairs)  30.2 us
    all_to_all x9, waiting for transfers between devices, exchange(): return lax.all_to_all(copies, axis, split_axis=0, concat_axis=0, tiled=True)  15.7 us
    gather x1, local copies, waits for them, and re-layouts, shards(): targets.at[ordering].get(unique_indices=True, mode='promise_in_bounds')  4.1 us
  transfers between devices with their start and end apart: 33, of which 7 were waited for; matrix products, arithmetic and copies ran while one was open for 3% of the time, Pallas kernels for 28%

profile of v2, /device:TPU:1, one launch (start us, length us, event | category | flops | bytes accessed | tf_op | source)
XLA Modules:
  0.0 185.1 jit_solution(14471358727423587575)
XLA Ops:
  0.6 2.5 %shard_map.87 = (f32[128,512]{1,0:T(8,128)}, f32[128,640]{1,0:T(8,128)}, f32[128,640]{1,0:T(8,128)}, f32[128,640]{1,0:T(8,128)}) custom-call(f32[128,2048]{1,0:T(8,128)} %row_ref.1, f32[128,128]{1,0:T(8,128)} %top_ref.3), custom_call_target="tpu_custom_call" | custom-call | bytes 2359296 | tf_op jit(solution)/shard_map/pallas_call | solution.py:40
  5.3 2.6 %collective-permute-start.1 = (f32[128,640]{1,0:T(8,128)}, f32[128,640]{1,0:T(8,128)S(1)}, u32[]{:S(2)}, u32[]{:S(2)}) collective-permute-start(f32[128,640]{1,0:T(8,128)} %get-tuple-element.38), channel_id=1, source_target_pairs={{0,8},{1,9},{2,10},{3,11},{4,12},{5,13},{6,14},{7,15},{8,0},{9,1},... | collective-permute-start | bytes 983048 | tf_op jit(solution)/shard_map/ppermute | solution.py:59
  9.7 4.1 %gather_fusion = f32[1280,256]{1,0:T(8,128)} fusion(f32[1280,256]{1,0:T(8,128)S(1)} %copy-done, s32[2048]{0:T(1024)S(1)} %pad_clamp_fusion), kind=kCustom, calls=%fused_computation | custom fusion | bytes 2626560 | tf_op jit(solution)/shard_map/gather | solution.py:479
  13.8 3.9 %shard_map.86 = (bf16[2,1280,256]{2,1,0:T(8,128)(2,1)}, f32[128,256]{1,0:T(8,128)}, f32[256,128]{1,0:T(8,128)}) custom-call(f32[1280,256]{1,0:T(8,128)} %gather_fusion, f32[1280,128]{1,0:T(8,128)} %basis_ref.1, f32[128,128]{1,0:T(8,128)S(1)} %copy-done.2), custom_call_target="tpu_custom_call" | custom-call | flops 754974720 | bytes 3604480 | tf_op jit(solution)/shard_map/pallas_call | solution.py:40
  17.8 2.6 %collective-permute-start.5 = (f32[128,256]{1,0:T(8,128)}, f32[128,256]{1,0:T(8,128)S(1)}, u32[]{:S(2)}, u32[]{:S(2)}) collective-permute-start(f32[128,256]{1,0:T(8,128)} %get-tuple-element.41.refs_0_), channel_id=1, source_target_pairs={{0,3},{1,0},{2,1},{3,2},{4,7},{5,4},{6,5},{7,6},{8,11},{9,8},{10,9... | collective-permute-start | bytes 393224 | tf_op jit(solution)/shard_map/ppermute | solution.py:59
  24.4 2.5 %collective-permute-start.11 = (f32[4,128,128]{2,1,0:T(8,128)}, f32[4,128,128]{2,1,0:T(8,128)S(1)}, u32[]{:S(2)}, u32[]{:S(2)}) collective-permute-start(f32[4,128,128]{2,1,0:T(8,128)} %get-tuple-element.47.refs_0_), channel_id=1, source_target_pairs={{0,3},{1,0},{2,1},{3,2},{4,7},{5,4},{6,5},{7,6},{8,11},{9,8},{10,9... | collective-permute-start | bytes 786440 | tf_op jit(solution)/shard_map/ppermute | solution.py:59
  26.9 4.5 %all-to-all-start = ((f32[16,16,128]{2,1,0:T(8,128)}), f32[16,16,128]{2,1,0:T(8,128)S(1)}, u32[]{:S(2)}, u32[]{:S(2)}) async-start(f32[16,16,128]{2,1,0:T(8,128)} %bitcast.1), calls=%async_computation | async-start | bytes 262144 | tf_op jit(solution)/shard_map/all_to_all | solution.py:50
  31.4 3.0 %collective-permute-start.4 = (f32[128,256]{1,0:T(8,128)S(1)}, f32[128,256]{1,0:T(8,128)S(1)}, u32[]{:S(2)}, u32[]{:S(2)}) collective-permute-start(f32[128,256]{1,0:T(8,128)S(1)} %copy-done.3), channel_id=1, source_target_pairs={{0,2},{1,3},{2,0},{3,1},{4,6},{5,7},{6,4},{7,5},{8,10},{9,11},{10,... | collective-permute-start | bytes 393224 | tf_op jit(solution)/shard_map/ppermute | solution.py:59
  38.9 11.9 %all-to-all-start.1 = ((f32[16,16,128]{2,1,0:T(8,128)}), f32[16,16,128]{2,1,0:T(8,128)S(1)}, u32[]{:S(2)}, u32[]{:S(2)}) async-start(f32[16,16,128]{2,1,0:T(8,128)} %shard_map.92), calls=%async_computation.1 | async-start | bytes 262144 | tf_op jit(solution)/shard_map/all_to_all | solution.py:50
  50.8 3.3 %shard_map.89 = (f32[128,256]{1,0:T(8,128)}, f32[128,256]{1,0:T(8,128)}, f32[128,256]{1,0:T(8,128)}, f32[128,256]{1,0:T(8,128)}) custom-call(bf16[2,512,512]{2,1,0:T(8,128)(2,1)} %get-tuple-element.40.split_ref, f32[128,256]{1,0:T(8,128)} %get-tuple-element.41.refs_0_, f32[128,256]{1,0:T(8,128)S(1)} %collective-permute-done.3.refs_1_, ...), custom_call_target="tpu_custom_call" | custom-call | flops 402653184 | bytes 2097152 | tf_op jit(solution)/shard_map/pallas_call | solution.py:40
  56.6 2.3 %shard_map.91.split_ref = bf16[2,16,128,128]{3,2,1,0:T(8,128)(2,1)} custom-call(f32[4,128,128]{2,1,0:T(8,128)} %get-tuple-element.47.refs_0_, f32[4,128,128]{2,1,0:T(8,128)S(1)} %collective-permute-done.9.refs_1_, f32[4,128,128]{2,1,0:T(8,128)S(1)} %collective-permute-done.10.refs_2_, f32[4,128,128]{2,1,0:T(8,128)S(1)} %collective-permute-done.11.refs_3_), custom_call_target="tpu_custom_call" | custom-call | bytes 2097152 | tf_op jit(solution)/shard_map/pallas_call | solution.py:40
  61.9 4.4 %all-to-all-start.2 = ((f32[16,16,128]{2,1,0:T(8,128)}), f32[16,16,128]{2,1,0:T(8,128)S(1)}, u32[]{:S(2)}, u32[]{:S(2)}) async-start(f32[16,16,128]{2,1,0:T(8,128)} %shard_map.93), calls=%async_computation.2 | async-start | bytes 262144 | tf_op jit(solution)/shard_map/all_to_all | solution.py:50
  66.3 8.3 %shard_map.90 = (f32[1280,256]{1,0:T(8,128)}, bf16[2,1280,1280]{2,1,0:T(8,128)(2,1)}) custom-call(f32[1280,256]{1,0:T(8,128)} %gather_fusion, f32[1280,1280]{1,0:T(8,128)} %refs_1_.1, bf16[2,1280,256]{2,1,0:T(8,128)(2,1)} %get-tuple-element.35.refs_2_.refs_3_, f32[128,256]{1,0:T(8,128)} %get-tuple-element.42.refs_3_, ...), custom_call_target="tpu_custom_call" | custom-call | flops 2516582400 | bytes 17563648 | tf_op jit(solution)/shard_map/pallas_call | solution.py:40
  74.7 4.8 %shard_map.94 = (f32[1280,256]{1,0:T(8,128)}, f32[128,256]{1,0:T(8,128)}, f32[256,128]{1,0:T(8,128)}) custom-call(f32[1280,256]{1,0:T(8,128)} %get-tuple-element.46.refs_0_, f32[1280,256]{1,0:T(8,128)} %gather_fusion, bf16[2,1280,256]{2,1,0:T(8,128)(2,1)} %get-tuple-element.35.refs_2_.refs_3_, f32[256,128]{1,0:T(8,128)S(1)} %bitcast.9), custom_call_target="tpu_custom_call" | custom-call | flops 754974720 | bytes 5636096 | tf_op jit(solution)/shard_map/pallas_call | solution.py:40
  79.5 6.7 %all-to-all-start.3 = ((f32[16,16,128]{2,1,0:T(8,128)}), f32[16,16,128]{2,1,0:T(8,128)S(1)}, u32[]{:S(2)}, u32[]{:S(2)}) async-start(f32[16,16,128]{2,1,0:T(8,128)} %bitcast.12), calls=%async_computation.3 | async-start | bytes 262144 | tf_op jit(solution)/shard_map/all_to_all | solution.py:50
  86.2 2.6 %collective-permute-start.14 = (f32[128,256]{1,0:T(8,128)}, f32[128,256]{1,0:T(8,128)S(1)}, u32[]{:S(2)}, u32[]{:S(2)}) collective-permute-start(f32[128,256]{1,0:T(8,128)} %get-tuple-element.51.refs_0_), channel_id=1, source_target_pairs={{0,3},{1,0},{2,1},{3,2},{4,7},{5,4},{6,5},{7,6},{8,11},{9,8},{10,9... | collective-permute-start | bytes 393224 | tf_op jit(solution)/shard_map/ppermute | solution.py:59
  89.9 3.1 %all-to-all-done.3.parts_ref = f32[16,16,128]{2,1,0:T(8,128)S(1)} async-done(((f32[16,16,128]{2,1,0:T(8,128)}), f32[16,16,128]{2,1,0:T(8,128)S(1)}, u32[]{:S(2)}, u32[]{:S(2)}) %all-to-all-start.3) | async-done | bytes 131104 | tf_op jit(solution)/shard_map/all_to_all | solution.py:50
  93.7 10.6 %all-to-all-start.4 = ((f32[16,16,128]{2,1,0:T(8,128)}), f32[16,16,128]{2,1,0:T(8,128)S(1)}, u32[]{:S(2)}, u32[]{:S(2)}) async-start(f32[16,16,128]{2,1,0:T(8,128)} %shard_map.97), calls=%async_computation.4 | async-start | bytes 262144 | tf_op jit(solution)/shard_map/all_to_all | solution.py:50
  104.3 3.2 %shard_map.95 = (f32[128,256]{1,0:T(8,128)}, f32[128,256]{1,0:T(8,128)}, f32[128,256]{1,0:T(8,128)}, f32[128,256]{1,0:T(8,128)}) custom-call(bf16[2,512,512]{2,1,0:T(8,128)(2,1)} %get-tuple-element.40.split_ref, f32[128,256]{1,0:T(8,128)} %get-tuple-element.51.refs_0_, f32[128,256]{1,0:T(8,128)S(1)} %collective-permute-done.12.refs_1_, ...), custom_call_target="tpu_custom_call" | custom-call | flops 402653184 | bytes 2097152 | tf_op jit(solution)/shard_map/pallas_call | solution.py:40
  109.1 4.1 %all-to-all-done.4.parts_ref = f32[16,16,128]{2,1,0:T(8,128)S(1)} async-done(((f32[16,16,128]{2,1,0:T(8,128)}), f32[16,16,128]{2,1,0:T(8,128)S(1)}, u32[]{:S(2)}, u32[]{:S(2)}) %all-to-all-start.4) | async-done | bytes 131104 | tf_op jit(solution)/shard_map/all_to_all | solution.py:50
  115.4 3.5 %all-to-all-start.5 = ((f32[16,16,128]{2,1,0:T(8,128)}), f32[16,16,128]{2,1,0:T(8,128)S(1)}, u32[]{:S(2)}, u32[]{:S(2)}) async-start(f32[16,16,128]{2,1,0:T(8,128)} %shard_map.98), calls=%async_computation.5 | async-start | bytes 262144 | tf_op jit(solution)/shard_map/all_to_all | solution.py:50
  118.9 8.2 %shard_map.96 = (f32[1280,256]{1,0:T(8,128)}, f32[1280,256]{1,0:T(8,128)}) custom-call(f32[1280,256]{1,0:T(8,128)} %gather_fusion, f32[1280,256]{1,0:T(8,128)} %get-tuple-element.49.refs_1_, bf16[2,1280,1280]{2,1,0:T(8,128)(2,1)} %get-tuple-element.50.refs_2_, bf16[2,1280,256]{2,1,0:T(8,128)(2,1)} %get-tuple-element.35.refs_2_.refs_3_, ...), custom_call_target="tpu_custom_call" | custom-call | flops 2516582400 | bytes 13631488 | tf_op jit(solution)/shard_map/pallas_call | solution.py:40
  127.2 4.8 %shard_map.99 = (f32[1280,256]{1,0:T(8,128)}, f32[128,256]{1,0:T(8,128)}, f32[256,128]{1,0:T(8,128)}) custom-call(f32[1280,256]{1,0:T(8,128)} %get-tuple-element.56.refs_0_, f32[1280,256]{1,0:T(8,128)} %get-tuple-element.57.refs_1_, bf16[2,1280,256]{2,1,0:T(8,128)(2,1)} %get-tuple-element.35.refs_2_.refs_3_, f32[256,128]{1,0:T(8,128)S(1)} %bitcast.8), custom_call_target="tpu_custom_call" | custom-call | flops 754974720 | bytes 5636096 | tf_op jit(solution)/shard_map/pallas_call | solution.py:40
  131.9 6.6 %all-to-all-start.6 = ((f32[16,16,128]{2,1,0:T(8,128)}), f32[16,16,128]{2,1,0:T(8,128)S(1)}, u32[]{:S(2)}, u32[]{:S(2)}) async-start(f32[16,16,128]{2,1,0:T(8,128)} %bitcast.11), calls=%async_computation.6 | async-start | bytes 262144 | tf_op jit(solution)/shard_map/all_to_all | solution.py:50
  138.5 2.6 %collective-permute-start.20 = (f32[128,256]{1,0:T(8,128)}, f32[128,256]{1,0:T(8,128)S(1)}, u32[]{:S(2)}, u32[]{:S(2)}) collective-permute-start(f32[128,256]{1,0:T(8,128)} %get-tuple-element.60.refs_0_), channel_id=1, source_target_pairs={{0,3},{1,0},{2,1},{3,2},{4,7},{5,4},{6,5},{7,6},{8,11},{9,8},{10,9... | collective-permute-start | bytes 393224 | tf_op jit(solution)/shard_map/ppermute | solution.py:59
  142.3 3.1 %all-to-all-done.6.parts_ref = f32[16,16,128]{2,1,0:T(8,128)S(1)} async-done(((f32[16,16,128]{2,1,0:T(8,128)}), f32[16,16,128]{2,1,0:T(8,128)S(1)}, u32[]{:S(2)}, u32[]{:S(2)}) %all-to-all-start.6) | async-done | bytes 131104 | tf_op jit(solution)/shard_map/all_to_all | solution.py:50
  146.1 8.5 %all-to-all-start.7 = ((f32[16,16,128]{2,1,0:T(8,128)}), f32[16,16,128]{2,1,0:T(8,128)S(1)}, u32[]{:S(2)}, u32[]{:S(2)}) async-start(f32[16,16,128]{2,1,0:T(8,128)} %shard_map.102), calls=%async_computation.7 | async-start | bytes 262144 | tf_op jit(solution)/shard_map/all_to_all | solution.py:50
  154.6 3.2 %shard_map.100 = (f32[128,256]{1,0:T(8,128)}, f32[128,256]{1,0:T(8,128)}, f32[128,256]{1,0:T(8,128)}, f32[128,256]{1,0:T(8,128)}) custom-call(bf16[2,512,512]{2,1,0:T(8,128)(2,1)} %get-tuple-element.40.split_ref, f32[128,256]{1,0:T(8,128)} %get-tuple-element.60.refs_0_, f32[128,256]{1,0:T(8,128)S(1)} %collective-permute-done.18.refs_1_, ...), custom_call_target="tpu_custom_call" | custom-call | flops 402653184 | bytes 2097152 | tf_op jit(solution)/shard_map/pallas_call | solution.py:40
  159.4 4.1 %all-to-all-done.7.parts_ref = f32[16,16,128]{2,1,0:T(8,128)S(1)} async-done(((f32[16,16,128]{2,1,0:T(8,128)}), f32[16,16,128]{2,1,0:T(8,128)S(1)}, u32[]{:S(2)}, u32[]{:S(2)}) %all-to-all-start.7) | async-done | bytes 131104 | tf_op jit(solution)/shard_map/all_to_all | solution.py:50
  165.7 3.5 %all-to-all-start.8 = ((f32[16,16,128]{2,1,0:T(8,128)}), f32[16,16,128]{2,1,0:T(8,128)S(1)}, u32[]{:S(2)}, u32[]{:S(2)}) async-start(f32[16,16,128]{2,1,0:T(8,128)} %shard_map.103), calls=%async_computation.8 | async-start | bytes 262144 | tf_op jit(solution)/shard_map/all_to_all | solution.py:50
  169.3 8.2 %shard_map.101 = (f32[1280,256]{1,0:T(8,128)}, f32[1280,256]{1,0:T(8,128)}) custom-call(f32[1280,256]{1,0:T(8,128)} %gather_fusion, f32[1280,256]{1,0:T(8,128)} %get-tuple-element.59.refs_1_, bf16[2,1280,1280]{2,1,0:T(8,128)(2,1)} %get-tuple-element.50.refs_2_, bf16[2,1280,256]{2,1,0:T(8,128)(2,1)} %get-tuple-element.35.refs_2_.refs_3_, ...), custom_call_target="tpu_custom_call" | custom-call | flops 2516582400 | bytes 13631488 | tf_op jit(solution)/shard_map/pallas_call | solution.py:40
  177.5 7.4 %shard_map.104 = (f32[1280,256]{1,0:T(8,128)}, f32[1280,256]{1,0:T(8,128)}) custom-call(f32[1280,256]{1,0:T(8,128)} %get-tuple-element.65.refs_0_, f32[1280,256]{1,0:T(8,128)} %get-tuple-element.66.refs_1_, bf16[2,1280,256]{2,1,0:T(8,128)(2,1)} %get-tuple-element.35.refs_2_.refs_3_, f32[256,128]{1,0:T(8,128)S(1)} %bitcast.10, s32[1,1280]{1,0:T(1,128)S(1)} %copy-done.1), custom_call_target="tpu_custom_call" | custom-call | flops 754974720 | bytes 6689792 | tf_op jit(solution)/shard_map/pallas_call | solution.py:40
  (64 shorter events, 29.2 us)
Async XLA Ops:
  3.2 17.2 %collective-permute-start = (f32[128,640]{1,0:T(8,128)}, f32[128,640]{1,0:T(8,128)S(1)}, u32[]{:S(2)}, u32[]{:S(2)}) collective-permute-start(f32[128,640]{1,0:T(8,128)} %get-tuple-element.37), channel_id=1, source_target_pairs={{0,4},{1,5},{2,6},{3,7},{4,8},{5,9},{6,10},{7,11},{8,12},{9,13},{1... | collective-permute-start | bytes 983048 | tf_op jit(solution)/shard_map/ppermute | solution.py:59
  5.3 17.0 %collective-permute-start.1 = (f32[128,640]{1,0:T(8,128)}, f32[128,640]{1,0:T(8,128)S(1)}, u32[]{:S(2)}, u32[]{:S(2)}) collective-permute-start(f32[128,640]{1,0:T(8,128)} %get-tuple-element.38), channel_id=1, source_target_pairs={{0,8},{1,9},{2,10},{3,11},{4,12},{5,13},{6,14},{7,15},{8,0},{9,1},... | collective-permute-start | bytes 983048 | tf_op jit(solution)/shard_map/ppermute | solution.py:59
  7.9 14.4 %collective-permute-start.2 = (f32[128,640]{1,0:T(8,128)}, f32[128,640]{1,0:T(8,128)S(1)}, u32[]{:S(2)}, u32[]{:S(2)}) collective-permute-start(f32[128,640]{1,0:T(8,128)} %get-tuple-element.39), channel_id=1, source_target_pairs={{0,12},{1,13},{2,14},{3,15},{4,0},{5,1},{6,2},{7,3},{8,4},{9,5},{1... | collective-permute-start | bytes 983048 | tf_op jit(solution)/shard_map/ppermute | solution.py:59
  17.8 18.6 %collective-permute-start.5 = (f32[128,256]{1,0:T(8,128)}, f32[128,256]{1,0:T(8,128)S(1)}, u32[]{:S(2)}, u32[]{:S(2)}) collective-permute-start(f32[128,256]{1,0:T(8,128)} %get-tuple-element.41.refs_0_), channel_id=1, source_target_pairs={{0,3},{1,0},{2,1},{3,2},{4,7},{5,4},{6,5},{7,6},{8,11},{9,8},{10,9... | collective-permute-start | bytes 393224 | tf_op jit(solution)/shard_map/ppermute | solution.py:59
  24.4 31.7 %collective-permute-start.11 = (f32[4,128,128]{2,1,0:T(8,128)}, f32[4,128,128]{2,1,0:T(8,128)S(1)}, u32[]{:S(2)}, u32[]{:S(2)}) collective-permute-start(f32[4,128,128]{2,1,0:T(8,128)} %get-tuple-element.47.refs_0_), channel_id=1, source_target_pairs={{0,3},{1,0},{2,1},{3,2},{4,7},{5,4},{6,5},{7,6},{8,11},{9,8},{10,9... | collective-permute-start | bytes 786440 | tf_op jit(solution)/shard_map/ppermute | solution.py:59
  26.9 11.3 %all-to-all-start = ((f32[16,16,128]{2,1,0:T(8,128)}), f32[16,16,128]{2,1,0:T(8,128)S(1)}, u32[]{:S(2)}, u32[]{:S(2)}) async-start(f32[16,16,128]{2,1,0:T(8,128)} %bitcast.1), calls=%async_computation | async-start | bytes 262144 | tf_op jit(solution)/shard_map/all_to_all | solution.py:50
  31.4 19.4 %collective-permute-start.4 = (f32[128,256]{1,0:T(8,128)S(1)}, f32[128,256]{1,0:T(8,128)S(1)}, u32[]{:S(2)}, u32[]{:S(2)}) collective-permute-start(f32[128,256]{1,0:T(8,128)S(1)} %copy-done.3), channel_id=1, source_target_pairs={{0,2},{1,3},{2,0},{3,1},{4,6},{5,7},{6,4},{7,5},{8,10},{9,11},{10,... | collective-permute-start | bytes 393224 | tf_op jit(solution)/shard_map/ppermute | solution.py:59
  34.3 16.5 %collective-permute-start.3 = (f32[128,256]{1,0:T(8,128)S(1)}, f32[128,256]{1,0:T(8,128)S(1)}, u32[]{:S(2)}, u32[]{:S(2)}) collective-permute-start(f32[128,256]{1,0:T(8,128)S(1)} %copy-done.3), channel_id=1, source_target_pairs={{0,1},{1,2},{2,3},{3,0},{4,5},{5,6},{6,7},{7,4},{8,9},{9,10},{10,1... | collective-permute-start | bytes 393224 | tf_op jit(solution)/shard_map/ppermute | solution.py:59
  34.6 22.0 %collective-permute-start.10 = (f32[4,128,128]{2,1,0:T(8,128)}, f32[4,128,128]{2,1,0:T(8,128)S(1)}, u32[]{:S(2)}, u32[]{:S(2)}) collective-permute-start(f32[4,128,128]{2,1,0:T(8,128)} %get-tuple-element.47.refs_0_), channel_id=1, source_target_pairs={{0,2},{1,3},{2,0},{3,1},{4,6},{5,7},{6,4},{7,5},{8,10},{9,11},{10,... | collective-permute-start | bytes 786440 | tf_op jit(solution)/shard_map/ppermute | solution.py:59
  36.4 20.2 %collective-permute-start.9 = (f32[4,128,128]{2,1,0:T(8,128)}, f32[4,128,128]{2,1,0:T(8,128)S(1)}, u32[]{:S(2)}, u32[]{:S(2)}) collective-permute-start(f32[4,128,128]{2,1,0:T(8,128)} %get-tuple-element.47.refs_0_), channel_id=1, source_target_pairs={{0,1},{1,2},{2,3},{3,0},{4,5},{5,6},{6,7},{7,4},{8,9},{9,10},{10,1... | collective-permute-start | bytes 786440 | tf_op jit(solution)/shard_map/ppermute | solution.py:59
  38.9 20.8 %all-to-all-start.1 = ((f32[16,16,128]{2,1,0:T(8,128)}), f32[16,16,128]{2,1,0:T(8,128)S(1)}, u32[]{:S(2)}, u32[]{:S(2)}) async-start(f32[16,16,128]{2,1,0:T(8,128)} %shard_map.92), calls=%async_computation.1 | async-start | bytes 262144 | tf_op jit(solution)/shard_map/all_to_all | solution.py:50
  54.1 12.3 %collective-permute-start.6 = (f32[128,256]{1,0:T(8,128)}, f32[128,256]{1,0:T(8,128)S(1)}, u32[]{:S(2)}, u32[]{:S(2)}) collective-permute-start(f32[128,256]{1,0:T(8,128)} %get-tuple-element.43), channel_id=1, source_target_pairs={{0,12},{1,13},{2,14},{3,15},{4,0},{5,1},{6,2},{7,3},{8,4},{9,5},{1... | collective-permute-start | bytes 393224 | tf_op jit(solution)/shard_map/ppermute | solution.py:59
  55.5 10.9 %collective-permute-start.7 = (f32[128,256]{1,0:T(8,128)}, f32[128,256]{1,0:T(8,128)S(1)}, u32[]{:S(2)}, u32[]{:S(2)}) collective-permute-start(f32[128,256]{1,0:T(8,128)} %get-tuple-element.44), channel_id=1, source_target_pairs={{0,8},{1,9},{2,10},{3,11},{4,12},{5,13},{6,14},{7,15},{8,0},{9,1},... | collective-permute-start | bytes 393224 | tf_op jit(solution)/shard_map/ppermute | solution.py:59
  56.0 10.3 %collective-permute-start.8 = (f32[128,256]{1,0:T(8,128)}, f32[128,256]{1,0:T(8,128)S(1)}, u32[]{:S(2)}, u32[]{:S(2)}) collective-permute-start(f32[128,256]{1,0:T(8,128)} %get-tuple-element.45), channel_id=1, source_target_pairs={{0,4},{1,5},{2,6},{3,7},{4,8},{5,9},{6,10},{7,11},{8,12},{9,13},{1... | collective-permute-start | bytes 393224 | tf_op jit(solution)/shard_map/ppermute | solution.py:59
  61.9 12.8 %all-to-all-start.2 = ((f32[16,16,128]{2,1,0:T(8,128)}), f32[16,16,128]{2,1,0:T(8,128)S(1)}, u32[]{:S(2)}, u32[]{:S(2)}) async-start(f32[16,16,128]{2,1,0:T(8,128)} %shard_map.93), calls=%async_computation.2 | async-start | bytes 262144 | tf_op jit(solution)/shard_map/all_to_all | solution.py:50
  79.5 13.5 %all-to-all-start.3 = ((f32[16,16,128]{2,1,0:T(8,128)}), f32[16,16,128]{2,1,0:T(8,128)S(1)}, u32[]{:S(2)}, u32[]{:S(2)}) async-start(f32[16,16,128]{2,1,0:T(8,128)} %bitcast.12), calls=%async_computation.3 | async-start | bytes 262144 | tf_op jit(solution)/shard_map/all_to_all | solution.py:50
  86.2 18.1 %collective-permute-start.14 = (f32[128,256]{1,0:T(8,128)}, f32[128,256]{1,0:T(8,128)S(1)}, u32[]{:S(2)}, u32[]{:S(2)}) collective-permute-start(f32[128,256]{1,0:T(8,128)} %get-tuple-element.51.refs_0_), channel_id=1, source_target_pairs={{0,3},{1,0},{2,1},{3,2},{4,7},{5,4},{6,5},{7,6},{8,11},{9,8},{10,9... | collective-permute-start | bytes 393224 | tf_op jit(solution)/shard_map/ppermute | solution.py:59
  88.7 15.6 %collective-permute-start.13 = (f32[128,256]{1,0:T(8,128)}, f32[128,256]{1,0:T(8,128)S(1)}, u32[]{:S(2)}, u32[]{:S(2)}) collective-permute-start(f32[128,256]{1,0:T(8,128)} %get-tuple-element.51.refs_0_), channel_id=1, source_target_pairs={{0,2},{1,3},{2,0},{3,1},{4,6},{5,7},{6,4},{7,5},{8,10},{9,11},{10,... | collective-permute-start | bytes 393224 | tf_op jit(solution)/shard_map/ppermute | solution.py:59
  89.3 15.0 %collective-permute-start.12 = (f32[128,256]{1,0:T(8,128)}, f32[128,256]{1,0:T(8,128)S(1)}, u32[]{:S(2)}, u32[]{:S(2)}) collective-permute-start(f32[128,256]{1,0:T(8,128)} %get-tuple-element.51.refs_0_), channel_id=1, source_target_pairs={{0,1},{1,2},{2,3},{3,0},{4,5},{5,6},{6,7},{7,4},{8,9},{9,10},{10,1... | collective-permute-start | bytes 393224 | tf_op jit(solution)/shard_map/ppermute | solution.py:59
  93.7 19.5 %all-to-all-start.4 = ((f32[16,16,128]{2,1,0:T(8,128)}), f32[16,16,128]{2,1,0:T(8,128)S(1)}, u32[]{:S(2)}, u32[]{:S(2)}) async-start(f32[16,16,128]{2,1,0:T(8,128)} %shard_map.97), calls=%async_computation.4 | async-start | bytes 262144 | tf_op jit(solution)/shard_map/all_to_all | solution.py:50
  107.5 11.4 %collective-permute-start.15 = (f32[128,256]{1,0:T(8,128)}, f32[128,256]{1,0:T(8,128)S(1)}, u32[]{:S(2)}, u32[]{:S(2)}) collective-permute-start(f32[128,256]{1,0:T(8,128)} %get-tuple-element.53), channel_id=1, source_target_pairs={{0,12},{1,13},{2,14},{3,15},{4,0},{5,1},{6,2},{7,3},{8,4},{9,5},{1... | collective-permute-start | bytes 393224 | tf_op jit(solution)/shard_map/ppermute | solution.py:59
  108.2 10.7 %collective-permute-start.16 = (f32[128,256]{1,0:T(8,128)}, f32[128,256]{1,0:T(8,128)S(1)}, u32[]{:S(2)}, u32[]{:S(2)}) collective-permute-start(f32[128,256]{1,0:T(8,128)} %get-tuple-element.54), channel_id=1, source_target_pairs={{0,8},{1,9},{2,10},{3,11},{4,12},{5,13},{6,14},{7,15},{8,0},{9,1},... | collective-permute-start | bytes 393224 | tf_op jit(solution)/shard_map/ppermute | solution.py:59
  115.4 11.8 %all-to-all-start.5 = ((f32[16,16,128]{2,1,0:T(8,128)}), f32[16,16,128]{2,1,0:T(8,128)S(1)}, u32[]{:S(2)}, u32[]{:S(2)}) async-start(f32[16,16,128]{2,1,0:T(8,128)} %shard_map.98), calls=%async_computation.5 | async-start | bytes 262144 | tf_op jit(solution)/shard_map/all_to_all | solution.py:50
  131.9 13.5 %all-to-all-start.6 = ((f32[16,16,128]{2,1,0:T(8,128)}), f32[16,16,128]{2,1,0:T(8,128)S(1)}, u32[]{:S(2)}, u32[]{:S(2)}) async-start(f32[16,16,128]{2,1,0:T(8,128)} %bitcast.11), calls=%async_computation.6 | async-start | bytes 262144 | tf_op jit(solution)/shard_map/all_to_all | solution.py:50
  138.5 16.1 %collective-permute-start.20 = (f32[128,256]{1,0:T(8,128)}, f32[128,256]{1,0:T(8,128)S(1)}, u32[]{:S(2)}, u32[]{:S(2)}) collective-permute-start(f32[128,256]{1,0:T(8,128)} %get-tuple-element.60.refs_0_), channel_id=1, source_target_pairs={{0,3},{1,0},{2,1},{3,2},{4,7},{5,4},{6,5},{7,6},{8,11},{9,8},{10,9... | collective-permute-start | bytes 393224 | tf_op jit(solution)/shard_map/ppermute | solution.py:59
  141.1 13.5 %collective-permute-start.19 = (f32[128,256]{1,0:T(8,128)}, f32[128,256]{1,0:T(8,128)S(1)}, u32[]{:S(2)}, u32[]{:S(2)}) collective-permute-start(f32[128,256]{1,0:T(8,128)} %get-tuple-element.60.refs_0_), channel_id=1, source_target_pairs={{0,2},{1,3},{2,0},{3,1},{4,6},{5,7},{6,4},{7,5},{8,10},{9,11},{10,... | collective-permute-start | bytes 393224 | tf_op jit(solution)/shard_map/ppermute | solution.py:59
  141.7 12.9 %collective-permute-start.18 = (f32[128,256]{1,0:T(8,128)}, f32[128,256]{1,0:T(8,128)S(1)}, u32[]{:S(2)}, u32[]{:S(2)}) collective-permute-start(f32[128,256]{1,0:T(8,128)} %get-tuple-element.60.refs_0_), channel_id=1, source_target_pairs={{0,1},{1,2},{2,3},{3,0},{4,5},{5,6},{6,7},{7,4},{8,9},{9,10},{10,1... | collective-permute-start | bytes 393224 | tf_op jit(solution)/shard_map/ppermute | solution.py:59
  146.1 17.4 %all-to-all-start.7 = ((f32[16,16,128]{2,1,0:T(8,128)}), f32[16,16,128]{2,1,0:T(8,128)S(1)}, u32[]{:S(2)}, u32[]{:S(2)}) async-start(f32[16,16,128]{2,1,0:T(8,128)} %shard_map.102), calls=%async_computation.7 | async-start | bytes 262144 | tf_op jit(solution)/shard_map/all_to_all | solution.py:50
  157.8 11.4 %collective-permute-start.21 = (f32[128,256]{1,0:T(8,128)}, f32[128,256]{1,0:T(8,128)S(1)}, u32[]{:S(2)}, u32[]{:S(2)}) collective-permute-start(f32[128,256]{1,0:T(8,128)} %get-tuple-element.62), channel_id=1, source_target_pairs={{0,12},{1,13},{2,14},{3,15},{4,0},{5,1},{6,2},{7,3},{8,4},{9,5},{1... | collective-permute-start | bytes 393224 | tf_op jit(solution)/shard_map/ppermute | solution.py:59
  158.5 10.8 %collective-permute-start.22 = (f32[128,256]{1,0:T(8,128)}, f32[128,256]{1,0:T(8,128)S(1)}, u32[]{:S(2)}, u32[]{:S(2)}) collective-permute-start(f32[128,256]{1,0:T(8,128)} %get-tuple-element.63), channel_id=1, source_target_pairs={{0,8},{1,9},{2,10},{3,11},{4,12},{5,13},{6,14},{7,15},{8,0},{9,1},... | collective-permute-start | bytes 393224 | tf_op jit(solution)/shard_map/ppermute | solution.py:59
  159.2 10.1 %collective-permute-start.23 = (f32[128,256]{1,0:T(8,128)}, f32[128,256]{1,0:T(8,128)S(1)}, u32[]{:S(2)}, u32[]{:S(2)}) collective-permute-start(f32[128,256]{1,0:T(8,128)} %get-tuple-element.64), channel_id=1, source_target_pairs={{0,4},{1,5},{2,6},{3,7},{4,8},{5,9},{6,10},{7,11},{8,12},{9,13},{1... | collective-permute-start | bytes 393224 | tf_op jit(solution)/shard_map/ppermute | solution.py:59
  165.7 11.8 %all-to-all-start.8 = ((f32[16,16,128]{2,1,0:T(8,128)}), f32[16,16,128]{2,1,0:T(8,128)S(1)}, u32[]{:S(2)}, u32[]{:S(2)}) async-start(f32[16,16,128]{2,1,0:T(8,128)} %shard_map.103), calls=%async_computation.8 | async-start | bytes 262144 | tf_op jit(solution)/shard_map/all_to_all | solution.py:50
  (5 other events, 45.1 us)
